TPU v7x, 128 devices: a whole 4x4x4 slice. The times are simulated.
128 devices in a mesh: dp: 2 (over z_hi), seq: 32 (over y, x, core), tensor: 2 (over z_lo).
Axes of the slice: x: 4, y: 4, z: 4 (z_hi: 2, z_lo: 2; z = z_hi * 2 + z_lo), core: 2. Of those that a mesh axis runs over, the one named last changes fastest.
Arguments:
- queries: bfloat16 [2, 16384, 4096], P('dp', 'seq', 'tensor'), may hold values from -6 to 6
- keys: bfloat16 [2, 16384, 4096], P('dp', 'seq', 'tensor'), may hold values from -6 to 6
- values: bfloat16 [2, 16384, 4096], P('dp', 'seq', 'tensor'), may hold values from -40 to 40
- grad_out: bfloat16 [2, 16384, 4096], P('dp', 'seq', 'tensor'), may hold values from -48 to 48
- doc_lengths: int32 [2, 16], P('dp'), may hold values from 1 to 9216, 16384 in all within a row
- gain: float32 [4096], P('tensor'), may hold values from 0.1 to 1.9
Outputs:
- layer_out: bfloat16 [2, 16384, 4096], P('dp', 'seq', 'tensor')
- grad_queries: bfloat16 [2, 16384, 4096], P('dp', 'seq', 'tensor')
- grad_keys: bfloat16 [2, 16384, 4096], P('dp', 'seq', 'tensor')
- grad_values: bfloat16 [2, 16384, 4096], P('dp', 'seq', 'tensor')
- grad_gain: float32 [4096], P('tensor')
Inputs may be any that keep to these rules, and one draw needn't show every extreme that they name: `doc_lengths`: each row sums to 16384; in every sequence the longest document has exactly 9216 tokens.
All inputs are finite; a program needn't handle non-finite values.
Results may differ from a plain program's by a relative error of at most 0.0063.
Values may be sent and summed in bfloat16 or wider, within the bound.
No kernel may reach another device: no remote copies, remote signals or barrier semaphores. Data moves between devices by JAX's collectives and lax.ppermute only.
A program may use at most 128 MiB of HBM per device.

v0:
```python
import jax
import jax.numpy as jnp
from jax import lax
from jax.sharding import PartitionSpec as P

HEADS = 32
HD = 128


epsilon = 1e-05


def prefix(value, axis, join, neutral, backward):
    count = lax.axis_size(axis)
    place = lax.axis_index(axis)
    ahead = count - 1 - place if backward else place
    gathered = jax.tree.map(
        lambda a, kind: lax.all_gather(a.astype(kind), axis), value, (jnp.bfloat16, jnp.bfloat16)
    )
    state = jax.tree.map(lambda a, e: jnp.zeros_like(a) + jnp.asarray(e, a.dtype), value, neutral)

    def one(step, state):
        source = count - 1 - step if backward else step
        return join(
            state,
            jax.tree.map(
                lambda a, own: lax.dynamic_index_in_dim(a, source, 0, False).astype(own.dtype),
                gathered,
                value,
            ),
        )

    return lax.fori_loop(0, ahead, one, state)


def linked(earlier, later):
    keeping = 1.0 - later[1][0]
    return (later[0] + keeping * earlier[0], jnp.maximum(earlier[1], later[1]))


def carried(state, flags, backward):
    blank = jnp.zeros(state.shape, jnp.float32)
    total, unused = prefix(
        (state.astype(jnp.float32), flags),
        "seq",
        linked,
        (blank, jnp.zeros((1,), jnp.float32)),
        backward,
    )
    return total


def head_major(array, shape):
    return jnp.transpose(array.reshape(shape), (1, 0, 2))


def body(queries, keys, values, grad_out, doc_lengths, gain):
    count = queries.shape[1]
    local_width = queries.shape[2]
    local_heads = local_width // HD
    shape = (count, local_heads, HD)
    query = head_major(queries[0], shape)
    key = head_major(keys[0], shape)
    value = head_major(values[0], shape)
    lengths = doc_lengths[0]
    starts = jnp.cumsum(lengths) - lengths
    block = lax.axis_index("seq")
    begin = block * count
    position = begin + jnp.arange(count, dtype=jnp.int32)
    document = jnp.sum((starts[None, :] <= position[:, None]).astype(jnp.int32), axis=1) - 1
    first_doc = document[0]
    last_doc = document[-1]
    numbers = jnp.arange(starts.shape[0], dtype=jnp.int32)
    last_end = jnp.sum(jnp.where(numbers == last_doc, starts + lengths, 0))
    last_block = (last_end - 1) // count
    continues = jnp.logical_not(jnp.any(starts == begin))
    starts_here = jnp.any((starts >= begin) & (starts < begin + count))
    flags = starts_here.astype(jnp.float32).reshape(1)
    first_mask = (document == first_doc) & continues
    last_mask = document == last_doc
    indices = jnp.arange(count, dtype=jnp.int32)
    same = (indices[:, None] >= indices[None, :]) & (document[:, None] == document[None, :])
    key_last = jnp.where(last_mask[None, :, None], key, 0)
    value_last = jnp.where(last_mask[None, :, None], value, 0)
    query_first = jnp.where(first_mask[None, :, None], query, 0)
    state = jnp.einsum("htd,hte->hde", key_last, value, preferred_element_type=jnp.float32).astype(
        jnp.bfloat16
    )
    incoming = carried(state, flags, False)
    carry_in = jnp.where(continues, incoming, 0.0).astype(jnp.bfloat16)
    scores = jnp.einsum("htd,hsd->hts", query, key, preferred_element_type=jnp.float32)
    scores = jnp.where(same[None], scores, 0.0).astype(jnp.bfloat16)
    attended = jnp.einsum("hts,hsd->htd", scores, value, preferred_element_type=jnp.float32)
    attended = attended + jnp.einsum(
        "htd,hde->hte", query_first, carry_in, preferred_element_type=jnp.float32
    )
    attended = jnp.transpose(attended, (1, 0, 2)).reshape(count, local_width)
    squares = lax.psum(jnp.sum(attended * attended, axis=1), "tensor")
    rscale = lax.rsqrt(squares / (HEADS * HD) + epsilon)
    unit = attended * rscale[:, None]
    layer_out = (gain * unit).astype(jnp.bfloat16)
    upstream = grad_out[0].astype(jnp.float32)
    scaled = upstream * gain
    inner = lax.psum(jnp.sum(scaled * unit, axis=1), "tensor") / (HEADS * HD)
    grad_gain = lax.psum(jnp.sum(upstream * unit, axis=0), ("dp", "seq"))
    d_att = head_major(
        (rscale[:, None] * (scaled - unit * inner[:, None])).astype(jnp.bfloat16), shape
    )
    d_first = jnp.where(first_mask[None, :, None], d_att, 0)
    back_state = jnp.einsum(
        "htd,hte->hde", query_first, d_att, preferred_element_type=jnp.float32
    ).astype(jnp.bfloat16)
    outgoing = carried(back_state, flags, True)
    carry_back = jnp.where(last_block > block, outgoing, 0.0).astype(jnp.bfloat16)
    d_scores = jnp.einsum("hte,hse->hts", d_att, value, preferred_element_type=jnp.float32)
    d_scores = jnp.where(same[None], d_scores, 0.0).astype(jnp.bfloat16)
    grad_query = jnp.einsum("hts,hsd->htd", d_scores, key, preferred_element_type=jnp.float32)
    grad_query = grad_query + jnp.einsum(
        "hte,hde->htd", d_first, carry_in, preferred_element_type=jnp.float32
    )
    grad_key = jnp.einsum("hts,htd->hsd", d_scores, query, preferred_element_type=jnp.float32)
    grad_key = grad_key + jnp.einsum(
        "hse,hde->hsd", value_last, carry_back, preferred_element_type=jnp.float32
    )
    grad_value = jnp.einsum("hts,hte->hse", scores, d_att, preferred_element_type=jnp.float32)
    grad_value = grad_value + jnp.einsum(
        "hsd,hde->hse", key_last, carry_back, preferred_element_type=jnp.float32
    )
    out_shape = (1, count, local_width)

    def token_major(array):
        return jnp.transpose(array.astype(jnp.bfloat16), (1, 0, 2)).reshape(out_shape)

    return (
        layer_out.reshape(out_shape),
        token_major(grad_query),
        token_major(grad_key),
        token_major(grad_value),
        grad_gain,
    )


def solution(mesh):
    in_specs = (
        P("dp", "seq", "tensor"),
        P("dp", "seq", "tensor"),
        P("dp", "seq", "tensor"),
        P("dp", "seq", "tensor"),
        P("dp", None),
        P("tensor"),
    )
    out_specs = (
        P("dp", "seq", "tensor"),
        P("dp", "seq", "tensor"),
        P("dp", "seq", "tensor"),
        P("dp", "seq", "tensor"),
        P("tensor"),
    )
    return jax.shard_map(body, mesh=mesh, in_specs=in_specs, out_specs=out_specs, check_vma=False)
```

profile of v0, /device:TPU:0, one launch (start us, length us, event | category | flops | bytes accessed | tf_op | source)
XLA Modules:
  0.0 547.0 jit_solution(15308874766064887949)
XLA Ops:
  11.5 3.9 copy.79
  15.4 2.9 copy.82
  19.6 3.1 fusion.16
  24.8 69.2 %all-reduce = bf16[32]{0:T(256)(128)(2,1)S(1)} all-reduce(bf16[32]{0:T(256)(128)(2,1)S(1)} %dynamic-update-slice), channel_id=1, replica_groups=mesh['dp'=2,'seq'=32,'tensor'=2] {'seq'}, use_global_device_ids=true, to_apply=%add | all-reduce | flops 32 | bytes 128
  94.1 2.9 copy.78
  97.0 4.1 copy.87
  101.3 4.2 select_convert_fusion.1
  105.5 3.2 copy-done.1
  108.7 4.8 fusion.40
  113.6 5.0 fusion.7
  118.6 5.0 psum.21
  123.6 5.4 copy.88
  129.0 4.0 fusion.2
  133.0 5.1 psum.22
  138.2 4.3 fusion.8
  147.3 5.4 copy.86
  152.7 4.8 select_convert_fusion
  157.6 4.8 fusion.41
  162.4 4.3 add_convert_fusion.2
  166.7 3.9 copy.96
  170.6 252.2 %psum.23 = f32[2048]{0:T(1024)} all-reduce(f32[2048]{0:T(1024)S(1)} %get-tuple-element.155), channel_id=1, replica_groups=mesh['dp'=2,'seq'=32,'tensor'=2] {'dp','seq'}, use_global_device_ids=true, to_apply=%region_14.15 | all-reduce | flops 2048 | bytes 16384 | tf_op jit(solution)/shard_map/psum | solution.py:105
  422.8 3.9 multiply_convert_fusion
  426.7 6.7 %fusion.42 = f32[16,512,128]{1,2,0:T(8,128)} fusion(bf16[16,512,128]{1,2,0:T(8,128)(2,1)S(1)} %bitcast.105, bf16[16,512,512]{2,1,0:T(8,128)(2,1)} %copy-done), kind=kOutput, calls=%fused_computation.74 | convolution fusion | flops 1073741824 | bytes 14680064 | tf_op jit(solution)/shard_map/hts,htd->hsd/dot_general | solution.py:121
  433.5 86.6 %while.27 = (s32[]{:T(128)}, f32[16,128,128]{2,1,0:T(8,128)S(1)}, s32[]{:T(128)}, bf16[32,16,128,128]{3,2,1,0:T(8,128)(2,1)}, bf16[32,1]{0,1:T(2,128)(2,1)S(1)},...) while((s32[]{:T(128)}, f32[16,128,128]{2,1,0:T(8,128)S(1)}, s32[]{:T(128)}, ...), condition=%wide.region_12.13_spmd, body=%wide.region_11.12_spmd.sunk | while | flops 786439 | bytes 2621605 | solution.py:33
  434.2 2.1 convert_add_fusion.5
  437.0 2.1 convert_add_fusion.5
  439.8 2.1 convert_add_fusion.5
  442.6 2.1 convert_add_fusion.5
  521.8 6.2 %add_convert_fusion = bf16[16,512,128]{1,2,0:T(8,128)(2,1)} fusion(f32[16,512,128]{1,2,0:T(8,128)S(1)} %fusion.14, bf16[16,512,128]{1,2,0:T(8,128)(2,1)S(1)} %copy-done.9, bf16[16,512,512]{2,1,0:T(8,128)(2,1)} %copy-done.1), kind=kOutput, calls=%fused_computation.18 | convolution fusion | flops 1075838976 | bytes 16777216 | tf_op jit(solution)/shard_map/hts,hte->hse/dot_general | solution.py:125
  528.0 4.1 copy.98
  532.1 4.2 add_convert_fusion.1
  536.3 3.9 copy.97
  (109 shorter events, 90.0 us)
Async XLA Ops:
  7.2 106.3 %all-gather.5.cloned.1.call-start = ((), (), s32[]{:S(2)}) async-start(), calls=%async_computation | async-start | bytes 17301504 | tf_op jit(solution)/shard_map/all_gather | solution.py:18
  18.3 4.5 copy-start.2
  19.6 3.9 copy-start.11
  22.8 410.6 %all-gather.7.cloned.1.call-start = ((), (), s32[]{:S(2)}) async-start(), calls=%async_computation.1 | async-start | bytes 17301504 | tf_op jit(solution)/shard_map/all_gather | solution.py:18
  101.3 7.4 %copy-start.3 = (bf16[1,512,2048]{1,2,0:T(8,128)(2,1)S(1)}, bf16[1,512,2048]{1,2,0:T(8,128)(2,1)}, u32[]{:S(2)}) copy-start(bf16[1,512,2048]{1,2,0:T(8,128)(2,1)} %copy-done.2) | copy-start | bytes 6291460
  105.5 3.2 copy-start.1
  123.6 5.4 copy-start.10
  142.4 1.4 copy-start.7
  152.7 4.8 copy-start.5
  157.6 4.8 copy-start
  157.6 4.8 copy-start.8
  433.5 86.7 %copy-start.6 = (bf16[1,512,2048]{1,2,0:T(8,128)(2,1)S(1)}, bf16[1,512,2048]{1,2,0:T(8,128)(2,1)}, u32[]{:S(2)}) copy-start(bf16[1,512,2048]{1,2,0:T(8,128)(2,1)} %copy.79) | copy-start | bytes 6291460
  520.2 1.6 copy-start.9
  528.0 4.1 copy-start.4
Sparse Core Ops, SparseCore 0:
  22.9 75.2 all-gather.4
  145.5 151.3 all-gather.6
where the time goes:
time: 550 us; the launch traced here: 547 us
  blocking collectives  332 us (60%)
  other arithmetic  103 us (19%)
  matrix products  50.3 us (9%)
  local copies, waits for them, and re-layouts  44.8 us (8%)
  between operations  16.2 us (3%)
    psum x1, blocking collectives, body(): grad_gain = lax.psum(jnp.sum(upstream * unit, axis=0), ('dp', 'seq'))  252 us
    unnamed x1, blocking collectives  69.2 us
    add x31, other arithmetic, linked(): return (later[0] + keeping * earlier[0], jnp.maximum(earlier[1], later[1]))  65.4 us
    unnamed x33, local copies, waits for them, and re-layouts  28.3 us
    sub x31, other arithmetic, linked(): keeping = 1.0 - later[1][0]  20.3 us
  transfers between devices with their start and end apart: 2, of which 0 were waited for; matrix products, arithmetic and copies ran while one was open for 10% of the time, Pallas kernels for 0%

commit v1 on v0

v1 whole, which is shorter than its diff:
```python
import functools

import jax
import jax.numpy as jnp
from jax import lax
from jax.experimental import pallas as pl
from jax.experimental.pallas import tpu as pltpu
from jax.sharding import PartitionSpec as P

HEADS = 32
HD = 128
TOK = 512
HALF = 256
N_SEQ = 32
SLICE = 64
GG_ROWS = 32
GROUP = 4
EPS = 1e-05

F32 = jnp.float32
BF16 = jnp.bfloat16
NN = (((1,), (0,)), ((), ()))
NT = (((1,), (1,)), ((), ()))
TN = (((0,), (0,)), ((), ()))


def mm(a, b, dims):
    return lax.dot_general(a, b, dims, preferred_element_type=F32)


def local_starts(lens):
    begin = lax.axis_index("seq") * TOK
    total = -begin
    starts = []
    for d in range(lens.shape[1]):
        starts.append(total)
        total = total + lens[0, d]
    return starts


def first_end(starts):
    end = jnp.int32(TOK)
    fresh = jnp.int32(0)
    for s in reversed(starts):
        end = jnp.where(s > 0, s, end)
        fresh = jnp.where(s == 0, 1, fresh)
    end = jnp.minimum(end, TOK)
    return jnp.where(fresh == 1, 0, end)


def last_start(starts):
    begin = jnp.int32(0)
    for s in starts:
        begin = jnp.where(s <= TOK - 1, s, begin)
    return jnp.maximum(begin, 0)


def rows_before(limit):
    t = lax.broadcasted_iota(jnp.int32, (TOK, HD), 0)
    return jnp.where(t < limit, 1.0, 0.0).astype(BF16)


def rows_from(limit):
    t = lax.broadcasted_iota(jnp.int32, (TOK, HD), 0)
    return jnp.where(t >= limit, 1.0, 0.0).astype(BF16)


def keeps(lens):
    bits = jnp.int32(0)
    total = jnp.int32(0)
    for d in range(lens.shape[1]):
        bits = bits | lax.shift_left(jnp.int32(1), lax.shift_right_logical(total, 9))
        total = total + lens[0, d]
    return [
        (1 - (lax.shift_right_logical(bits, b) & 1)).astype(F32) for b in range(N_SEQ)
    ]


def cols(g):
    return slice(g * HD, (g + 1) * HD)


def state_kernel(lens, k, v, out, mask):
    @pl.when(pl.program_id(0) == 0)
    def _():
        mask[...] = rows_from(last_start(local_starts(lens)))

    for g in range(GROUP):
        kl = k[:, cols(g)] * mask[...]
        out[cols(g), :] = mm(kl, v[:, cols(g)], TN).astype(BF16)


def scan_kernel(lens, x, out):
    keep = keeps(lens)
    acc = jnp.zeros((SLICE, HD), F32)
    for b in range(N_SEQ):
        rows = slice(b * SLICE, (b + 1) * SLICE)
        out[rows, :] = acc.astype(BF16)
        acc = x[rows, :].astype(F32) + keep[b] * acc


def scan_back_kernel(lens, x, out, gg):
    keep = keeps(lens)
    acc = jnp.zeros((SLICE, HD), F32)
    step = SLICE + GG_ROWS
    for b in reversed(range(N_SEQ)):
        out[b * SLICE:(b + 1) * SLICE, :] = acc.astype(BF16)
        acc = x[b * step:b * step + SLICE, :].astype(F32) + keep[b] * acc
    high = jnp.zeros((GG_ROWS // 2, HD), F32)
    low = jnp.zeros((GG_ROWS // 2, HD), F32)
    for b in range(N_SEQ):
        base = b * step + SLICE
        high = high + x[base:base + GG_ROWS // 2, :].astype(F32)
        low = low + x[base + GG_ROWS // 2:base + GG_ROWS, :].astype(F32)
    gg[...] = high + low


def build_masks(lens, mask, mask_t):
    starts = local_starts(lens)
    t = lax.broadcasted_iota(jnp.int32, (TOK, HD), 0)
    lane = lax.broadcasted_iota(jnp.int32, (TOK, HD), 1)
    begin = jnp.zeros((TOK, HD), jnp.int32)
    for s in starts:
        begin = jnp.where(t >= s, jnp.maximum(s, 0), begin)
    end = jnp.full((TOK, HD), TOK, jnp.int32)
    for s in reversed(starts):
        end = jnp.where(s > t, jnp.minimum(s, TOK), end)
    for c in range(TOK // HD):
        s = lane + c * HD
        mask[:, cols(c)] = jnp.where((s <= t) & (s >= begin), 1.0, 0.0).astype(BF16)
        mask_t[:, cols(c)] = jnp.where((s >= t) & (s < end), 1.0, 0.0).astype(BF16)


def attend_head(q, k, v, mask, out, g):
    c = cols(g)
    for r in range(2):
        rows = slice(r * HALF, (r + 1) * HALF)
        wide = (r + 1) * HALF
        s = mm(q[rows, c], k[0:wide, c], NT).astype(BF16) * mask[rows, 0:wide]
        out[rows, c] = mm(s, v[0:wide, c], NN)


def attend_first_kernel(lens, q, k, v, out, mask, mask_t):
    @pl.when(pl.program_id(0) == 0)
    def _():
        build_masks(lens, mask, mask_t)

    for g in range(GROUP):
        attend_head(q, k, v, mask, out, g)


def attend_second_kernel(q, k, v, mask, unused, out):
    for g in range(GROUP):
        attend_head(q, k, v, mask, out, g)


def sums_kernel(lens, local, q, carry, up, gain, out, mask, squares, inners):
    i = pl.program_id(0)

    @pl.when(i == 0)
    def _():
        mask[...] = rows_before(first_end(local_starts(lens)))
        squares[...] = jnp.zeros((TOK, HD), F32)
        inners[...] = jnp.zeros((TOK, HD), F32)

    sq = squares[...]
    inn = inners[...]
    for g in range(GROUP):
        c = cols(g)
        att = local[:, c] + mm(q[:, c] * mask[...], carry[c, :], NN)
        sq = sq + att * att
        inn = inn + att * (up[:, c].astype(F32) * gain[:, c])
    squares[...] = sq
    inners[...] = inn

    @pl.when(i == pl.num_programs(0) - 1)
    def _():
        ones = jnp.ones((8, HD), F32)
        row = lax.broadcasted_iota(jnp.int32, (8, TOK), 0)
        one = lax.dot_general(ones, sq, NT, precision=lax.Precision.HIGHEST, preferred_element_type=F32)
        two = lax.dot_general(ones, inn, NT, precision=lax.Precision.HIGHEST, preferred_element_type=F32)
        out[...] = jnp.where(row == 0, one, two)


def norm_kernel(lens, mine, other, local, q, carry, up, gain,
                layer, d_att, send, mask, rscale, inner, gains):
    i = pl.program_id(0)

    @pl.when(i == 0)
    def _():
        mask[...] = rows_before(first_end(local_starts(lens)))
        both = jnp.transpose(mine[...] + other[...], (1, 0))
        scale = 1.0 / (HEADS * HD)
        rs = lax.rsqrt(jnp.broadcast_to(both[:, 0:1], (TOK, HD)) * scale + EPS)
        rscale[...] = rs
        inner[...] = rs * (jnp.broadcast_to(both[:, 1:2], (TOK, HD)) * scale)

    step = SLICE + GG_ROWS
    for g in range(GROUP):
        c = cols(g)
        qf = q[:, c] * mask[...]
        att = local[:, c] + mm(qf, carry[c, :], NN)
        unit = att * rscale[...]
        layer[:, c] = (gain[:, c] * unit).astype(BF16)
        upstream = up[:, c].astype(F32)
        gains[pl.ds(i * GROUP + g, 1), :] = jnp.sum(upstream * unit, axis=0, keepdims=True)
        da = (rscale[...] * (upstream * gain[:, c] - unit * inner[...])).astype(BF16)
        d_att[:, c] = da
        back = mm(qf, da, TN).astype(BF16)
        base = pl.multiple_of((i * GROUP + g) * (2 * step), 2 * step)
        send[pl.ds(base, SLICE), :] = back[0:SLICE, :]
        send[pl.ds(base + step, SLICE), :] = back[SLICE:HD, :]

    @pl.when(i == pl.num_programs(0) - 1)
    def _():
        total = gains[...]
        high = total.astype(BF16)
        low = (total - high.astype(F32)).astype(BF16)
        for b in range(N_SEQ):
            base = b * step + SLICE
            send[base:base + GG_ROWS // 2, :] = high
            send[base + GG_ROWS // 2:base + GG_ROWS, :] = low


def query_kernel(lens, d_att, k, v, carry, mask, out, first):
    @pl.when(pl.program_id(0) == 0)
    def _():
        first[...] = rows_before(first_end(local_starts(lens)))

    for g in range(GROUP):
        c = cols(g)
        for r in range(2):
            rows = slice(r * HALF, (r + 1) * HALF)
            wide = (r + 1) * HALF
            da = d_att[rows, c]
            ds = mm(da, v[0:wide, c], NT).astype(BF16) * mask[rows, 0:wide]
            gq = mm(ds, k[0:wide, c], NN) + mm(da * first[rows, :], carry[c, :], NT)
            out[rows, c] = gq.astype(BF16)


def local_kernel(q, k, v, d_att, mask_t, gk, gv):
    for g in range(GROUP):
        c = cols(g)
        for r in range(2):
            rows = slice(r * HALF, (r + 1) * HALF)
            at = slice(r * HALF, TOK)
            m = mask_t[rows, at]
            s = mm(k[rows, c], q[at, c], NT).astype(BF16) * m
            gv[rows, c] = mm(s, d_att[at, c], NN)
            ds = mm(v[rows, c], d_att[at, c], NT).astype(BF16) * m
            gk[rows, c] = mm(ds, q[at, c], NN)


def close_kernel(lens, gk_local, gv_local, k, v, carry, gg_mine, gg_other, gk, gv, gg, mask):
    @pl.when(pl.program_id(0) == 0)
    def _():
        mask[...] = rows_from(last_start(local_starts(lens)))
        gg[...] = gg_mine[...] + gg_other[...]

    for g in range(GROUP):
        c = cols(g)
        m = mask[...]
        gk[:, c] = (gk_local[:, c] + mm(v[:, c] * m, carry[c, :], NT)).astype(BF16)
        gv[:, c] = (gv_local[:, c] + mm(k[:, c] * m, carry[c, :], NN)).astype(BF16)


SMEM = pl.BlockSpec(memory_space=pltpu.SMEM)
VMEM_LIMIT = 40 * 1024 * 1024


def params():
    return pltpu.CompilerParams(dimension_semantics=("arbitrary",), vmem_limit_bytes=VMEM_LIMIT)


def tokens(first=0):
    return pl.BlockSpec((None, TOK, GROUP * HD), lambda i: (0, 0, i + first))


def flat(first=0):
    return pl.BlockSpec((TOK, GROUP * HD), lambda i: (0, i + first))


def whole(*shape):
    return pl.BlockSpec(shape, lambda i: (0,) * len(shape))


def head_rows():
    return pl.BlockSpec((GROUP * HD, HD), lambda i: (i, 0))


def gains_spec():
    return pl.BlockSpec((1, GROUP * HD), lambda i: (0, i))


def cost(flops, bytes_accessed):
    return pl.CostEstimate(flops=flops, transcendentals=0, bytes_accessed=bytes_accessed)


def struct(shape, dtype):
    return jax.ShapeDtypeStruct(shape, dtype)


def exchange(x, axis):
    return lax.ppermute(x, axis, [(0, 1), (1, 0)])


def swap(x):
    return lax.all_to_all(x, "seq", 0, 0, tiled=True)


def body(queries, keys, values, grad_out, doc_lengths, gain):
    width = queries.shape[2]
    heads = width // HD
    steps = heads // GROUP
    half = steps // 2
    gain = gain.reshape(1, width)
    lens = doc_lengths
    wide = struct((1, TOK, width), BF16)
    state_shape = (heads * HD, HD)
    column = lambda dtype: pltpu.VMEM((TOK, HD), dtype)
    mb = 1 << 20
    unit = 2 * heads * TOK * TOK * HD

    state = pl.pallas_call(
        state_kernel, grid=(steps,), name="state",
        in_specs=[SMEM, tokens(), tokens()], out_specs=head_rows(),
        out_shape=struct(state_shape, BF16), scratch_shapes=[column(BF16)],
        compiler_params=params(), cost_estimate=cost(unit // 4, 5 * mb),
    )(lens, keys, values)
    scattered = swap(state)
    local, mask, mask_t = pl.pallas_call(
        attend_first_kernel, grid=(half,), name="attend_first",
        in_specs=[SMEM, tokens(), tokens(), tokens()],
        out_specs=[flat(), whole(TOK, TOK), whole(TOK, TOK)],
        out_shape=[struct((TOK, width), F32), struct((TOK, TOK), BF16), struct((TOK, TOK), BF16)],
        compiler_params=params(), cost_estimate=cost(unit, 6 * mb),
    )(lens, queries, keys, values)
    summed = pl.pallas_call(
        scan_kernel, grid=(1,), name="scan",
        in_specs=[SMEM, whole(*state_shape)], out_specs=whole(*state_shape),
        out_shape=struct(state_shape, BF16),
        compiler_params=params(), cost_estimate=cost(mb, mb),
    )(lens, scattered)
    summed, local = lax.optimization_barrier((summed, local))
    carry_in = swap(summed)
    local = pl.pallas_call(
        attend_second_kernel, grid=(half,), name="attend_second",
        in_specs=[tokens(half), tokens(half), tokens(half), whole(TOK, TOK),
                  pl.BlockSpec(memory_space=pl.ANY)],
        out_specs=flat(half), out_shape=struct((TOK, width), F32),
        input_output_aliases={4: 0},
        compiler_params=params(), cost_estimate=cost(unit, 6 * mb),
    )(queries, keys, values, mask, local)
    sums = pl.pallas_call(
        sums_kernel, grid=(steps,), name="sums",
        in_specs=[SMEM, flat(), tokens(), head_rows(), tokens(), gains_spec()],
        out_specs=whole(8, TOK), out_shape=struct((8, TOK), F32),
        scratch_shapes=[column(BF16), column(F32), column(F32)],
        compiler_params=params(), cost_estimate=cost(unit // 4, 9 * mb),
    )(lens, local, queries, carry_in, grad_out, gain)
    other = exchange(sums, "tensor")
    step = SLICE + GG_ROWS
    send_shape = (N_SEQ * step, HD)
    layer_out, d_att, send = pl.pallas_call(
        norm_kernel, grid=(steps,), name="norm",
        in_specs=[SMEM, whole(8, TOK), whole(8, TOK), flat(), tokens(), head_rows(), tokens(),
                  gains_spec()],
        out_specs=[tokens(), flat(), whole(*send_shape)],
        out_shape=[wide, struct((TOK, width), BF16), struct(send_shape, BF16)],
        scratch_shapes=[column(BF16), column(F32), column(F32), pltpu.VMEM((heads, HD), F32)],
        compiler_params=params(), cost_estimate=cost(unit // 2, 13 * mb),
    )(lens, sums, other, local, queries, carry_in, grad_out, gain)
    back = swap(send)
    grad_queries = pl.pallas_call(
        query_kernel, grid=(steps,), name="grad_query",
        in_specs=[SMEM, flat(), tokens(), tokens(), head_rows(), whole(TOK, TOK)],
        out_specs=tokens(), out_shape=wide, scratch_shapes=[column(BF16)],
        compiler_params=params(), cost_estimate=cost(2 * unit, 9 * mb),
    )(lens, d_att, keys, values, carry_in, mask)
    back_sum, gg_mine = pl.pallas_call(
        scan_back_kernel, grid=(1,), name="scan_back",
        in_specs=[SMEM, whole(*send_shape)],
        out_specs=[whole(*state_shape), whole(GG_ROWS // 2, HD)],
        out_shape=[struct(state_shape, BF16), struct((GG_ROWS // 2, HD), F32)],
        compiler_params=params(), cost_estimate=cost(mb, mb),
    )(lens, back)
    back_sum, gg_mine, grad_queries, d_att = lax.optimization_barrier(
        (back_sum, gg_mine, grad_queries, d_att))
    carry_back = swap(back_sum)
    gg_other = exchange(gg_mine, "dp")
    gk_local, gv_local = pl.pallas_call(
        local_kernel, grid=(steps,), name="grad_local",
        in_specs=[tokens(), tokens(), tokens(), flat(), whole(TOK, TOK)],
        out_specs=[flat(), flat()],
        out_shape=[struct((TOK, width), F32), struct((TOK, width), F32)],
        compiler_params=params(), cost_estimate=cost(4 * unit, 16 * mb),
    )(queries, keys, values, d_att, mask_t)
    gg_shape = (GG_ROWS // 2, HD)
    grad_keys, grad_values, grad_gain = pl.pallas_call(
        close_kernel, grid=(steps,), name="grad_close",
        in_specs=[SMEM, flat(), flat(), tokens(), tokens(), head_rows(), whole(*gg_shape),
                  whole(*gg_shape)],
        out_specs=[tokens(), tokens(), whole(*gg_shape)],
        out_shape=[wide, wide, struct(gg_shape, F32)], scratch_shapes=[column(BF16)],
        compiler_params=params(), cost_estimate=cost(unit // 2, 17 * mb),
    )(lens, gk_local, gv_local, keys, values, carry_back, gg_mine, gg_other)
    return layer_out, grad_queries, grad_keys, grad_values, grad_gain.reshape(width)


def solution(mesh):
    spread = P("dp", "seq", "tensor")
    return jax.shard_map(
        body, mesh=mesh,
        in_specs=(spread, spread, spread, spread, P("dp", None), P("tensor")),
        out_specs=(spread, spread, spread, spread, P("tensor")),
        check_vma=False,
    )
```

time: 550 us -> 130 us (0.24)
  blocking collectives: 332 us -> 0 us
  other arithmetic: 103 us -> 0 us
  matrix products: 50.3 us -> 0 us
  Pallas kernels: 0 us -> 46 us
  starting transfers between devices: 0.08 us -> 31.2 us
  between operations: 16.2 us -> 0.8 us
  waiting for transfers between devices: 0.04 us -> 6.26 us
    psum x3 -> x0, blocking collectives: 262 us -> none  [the longest x1 252 us: body(): grad_gain = lax.psum(jnp.sum(upstream * unit, axis=0), ('dp', 'seq'))]
    unnamed x1 -> x0, blocking collectives: 69.2 us -> none
    add x32 -> x0, other arithmetic: 65.4 us -> none  [the longest x31 65.4 us: linked(): return (later[0] + keeping * earlier[0], jnp.maximum(earlier[1], later[1]))]
    dot_general x12 -> x0, matrix products: 50.3 us -> none  [the longest x1 6.69 us: body(): jnp.einsum('hts,htd->hsd', d_scores, query, preferred_element_type=jnp.fl...]
    pallas_call x0 -> x10, Pallas kernels: none -> 46 us  [the longest x1 11.5 us: body(): pl.pallas_call(local_kernel, grid=(steps,), name='grad_local', in_specs=[...]
    all_to_all x0 -> x4, starting transfers between devices: none -> 25.1 us  [swap(): return lax.all_to_all(x, 'seq', 0, 0, tiled=True)]
    sub x32 -> x0, other arithmetic: 20.3 us -> none  [the longest x31 20.3 us: linked(): keeping = 1.0 - later[1][0]]
    unnamed x33 -> x64, local copies, waits for them, and re-layouts: 28.3 us -> 43.4 us
  transfers between devices with their start and end apart: 2 -> 6, of which waited for: 0 -> 4; matrix products, arithmetic and copies ran while one was open for 10% -> 0% of each run, Pallas kernels for 0% -> 21%
where the time goes in v1:
time: 130 us; the launch traced here: 128 us
  Pallas kernels  46 us (35%)
  local copies, waits for them, and re-layouts  43.4 us (33%)
  starting transfers between devices  31.2 us (24%)
  waiting for transfers between devices  6.26 us (5%)
    unnamed x64, local copies, waits for them, and re-layouts  43.4 us
    all_to_all x4, starting transfers between devices, swap(): return lax.all_to_all(x, 'seq', 0, 0, tiled=True)  25.1 us
    pallas_call x1, Pallas kernels, body(): pl.pallas_call(local_kernel, grid=(steps,), name='grad_local', in_specs=[...  11.5 us
    pallas_call x1, Pallas kernels, body(): pl.pallas_call(query_kernel, grid=(steps,), name='grad_query', in_specs=[...  7.7 us
    ppermute x2, starting transfers between devices, exchange(): return lax.ppermute(x, axis, [(0, 1), (1, 0)])  6.13 us
    pallas_call x1, Pallas kernels, body(): pl.pallas_call(norm_kernel, grid=(steps,), name='norm', in_specs=[SMEM, w...  5.79 us
    pallas_call x1, Pallas kernels, body(): pl.pallas_call(attend_first_kernel, grid=(half,), name='attend_first', in...  4.72 us
    all_to_all x4, waiting for transfers between devices, swap(): return lax.all_to_all(x, 'seq', 0, 0, tiled=True)  4.46 us
  transfers between devices with their start and end apart: 6, of which 4 were waited for; matrix products, arithmetic and copies ran while one was open for 0% of the time, Pallas kernels for 21%

profile of v1, /device:TPU:0, one launch (start us, length us, event | category | flops | bytes accessed | tf_op | source)
XLA Modules:
  0.0 127.7 jit_solution(14095418517400006585)
XLA Ops:
  2.2 1.6 %copy-done.2 = bf16[1,512,2048]{2,1,0:T(8,128)(2,1)S(1)} copy-done((bf16[1,512,2048]{2,1,0:T(8,128)(2,1)S(1)}, bf16[1,512,2048]{2,1,0:T(8,128)(2,1)}, u32[]{:S(2)}) %copy-start.2) | copy-done | bytes 2097176
  4.5 3.2 %state.1 = bf16[2048,128]{1,0:T(8,128)(2,1)} custom-call(s32[1,16]{1,0:T(1,128)S(1)} %copy-done.28, bf16[1,512,2048]{2,1,0:T(8,128)(2,1)S(1)} %copy-done, bf16[1,512,2048]{2,1,0:T(8,128)(2,1)S(1)} %copy-done.2), custom_call_target="tpu_custom_call" | custom-call | flops 268435456 | bytes 5242880 | tf_op jit(solution)/shard_map/state/pallas_call | solution.py:324
  7.7 7.4 %all-to-all-start = ((bf16[32,64,128]{2,1,0:T(8,128)(2,1)}), bf16[32,64,128]{2,1,0:T(8,128)(2,1)S(1)}, u32[]{:S(2)}, u32[]{:S(2)}) async-start(bf16[32,64,128]{2,1,0:T(8,128)(2,1)} %bitcast), calls=%async_computation | async-start | bytes 1048576 | tf_op jit(solution)/shard_map/all_to_all | solution.py:308
  16.7 1.6 %copy-done.12 = bf16[1,512,2048]{2,1,0:T(8,128)(2,1)S(1)} copy-done((bf16[1,512,2048]{2,1,0:T(8,128)(2,1)S(1)}, bf16[1,512,2048]{2,1,0:T(8,128)(2,1)}, u32[]{:S(2)}) %copy-start.12) | copy-done | bytes 2097176
  18.3 4.7 %attend_first.1 = (f32[512,2048]{1,0:T(8,128)S(1)}, bf16[512,512]{1,0:T(8,128)(2,1)S(1)}, bf16[512,512]{1,0:T(8,128)(2,1)S(1)}) custom-call(s32[1,16]{1,0:T(1,128)S(1)} %copy-done.29, bf16[1,512,2048]{2,1,0:T(8,128)(2,1)S(1)} %copy-done.12, bf16[1,512,2048]{2,1,0:T(8,128)(2,1)S(1)} %copy-done.1, bf16[1,512,2048]{2,1,0:T(8,128)(2,1)S(1)} %copy-done.3), custom_call_target="tpu_custom_call" | custom-call | flops 1073741824 | bytes 6291456 | tf_op jit(solution)/shard_map/attend_first/pallas_call | solution.py:331
  23.1 1.9 %copy-done.8 = f32[512,2048]{1,0:T(8,128)} copy-done((f32[512,2048]{1,0:T(8,128)}, f32[512,2048]{1,0:T(8,128)S(1)}, u32[]{:S(2)}) %copy-start.8) | copy-done | bytes 4194328
  28.2 6.5 %all-to-all-start.1 = ((bf16[32,64,128]{2,1,0:T(8,128)(2,1)}), bf16[32,64,128]{2,1,0:T(8,128)(2,1)S(1)}, u32[]{:S(2)}, u32[]{:S(2)}) async-start(bf16[32,64,128]{2,1,0:T(8,128)(2,1)} %bitcast.2), calls=%async_computation.1 | async-start | bytes 1048576 | tf_op jit(solution)/shard_map/all_to_all | solution.py:308
  36.3 2.2 %copy-done.9 = f32[512,2048]{1,0:T(8,128)S(1)} copy-done((f32[512,2048]{1,0:T(8,128)S(1)}, f32[512,2048]{1,0:T(8,128)}, u32[]{:S(2)}) %copy-start.9) | copy-done | bytes 4194328
  38.5 1.6 %copy-done.13 = bf16[1,512,2048]{2,1,0:T(8,128)(2,1)S(1)} copy-done((bf16[1,512,2048]{2,1,0:T(8,128)(2,1)S(1)}, bf16[1,512,2048]{2,1,0:T(8,128)(2,1)}, u32[]{:S(2)}) %copy-start.13) | copy-done | bytes 2097176
  40.1 3.3 %attend_second.1.local = f32[512,2048]{1,0:T(8,128)S(1)} custom-call(bf16[1,512,2048]{2,1,0:T(8,128)(2,1)S(1)} %copy-done.13, bf16[1,512,2048]{2,1,0:T(8,128)(2,1)S(1)} %copy-done.1, bf16[1,512,2048]{2,1,0:T(8,128)(2,1)S(1)} %copy-done.4, bf16[512,512]{1,0:T(8,128)(2,1)S(1)} %get-tuple-element.24.mask, ...), custom_call_target="tpu_custom_call", output_to_operand_aliasing={{}: (4, {})} | custom-call | flops 1073741824 | bytes 6291456 | tf_op jit(solution)/shard_map/attend_second/pallas_call | solution.py:346
  43.4 1.9 %copy-done.10 = f32[512,2048]{1,0:T(8,128)} copy-done((f32[512,2048]{1,0:T(8,128)}, f32[512,2048]{1,0:T(8,128)S(1)}, u32[]{:S(2)}) %copy-start.10) | copy-done | bytes 4194328
  46.3 2.2 %copy-done.11 = f32[512,2048]{1,0:T(8,128)S(1)} copy-done((f32[512,2048]{1,0:T(8,128)S(1)}, f32[512,2048]{1,0:T(8,128)}, u32[]{:S(2)}) %copy-start.11) | copy-done | bytes 4194328
  48.5 1.6 %copy-done.14 = bf16[1,512,2048]{2,1,0:T(8,128)(2,1)S(1)} copy-done((bf16[1,512,2048]{2,1,0:T(8,128)(2,1)S(1)}, bf16[1,512,2048]{2,1,0:T(8,128)(2,1)}, u32[]{:S(2)}) %copy-start.14) | copy-done | bytes 2097176
  50.1 1.6 %copy-done.16 = bf16[1,512,2048]{2,1,0:T(8,128)(2,1)S(1)} copy-done((bf16[1,512,2048]{2,1,0:T(8,128)(2,1)S(1)}, bf16[1,512,2048]{2,1,0:T(8,128)(2,1)}, u32[]{:S(2)}) %copy-start.16) | copy-done | bytes 2097176
  51.7 3.2 %sums.1.mine = f32[8,512]{1,0:T(8,128)S(1)} custom-call(s32[1,16]{1,0:T(1,128)S(1)} %copy-done.29, f32[512,2048]{1,0:T(8,128)S(1)} %copy-done.11, bf16[1,512,2048]{2,1,0:T(8,128)(2,1)S(1)} %copy-done.14, bf16[2048,128]{1,0:T(8,128)(2,1)S(1)} %bitcast.10, bf16[1,512,2048]{2,1,0:T(8,128)(2,1)S(1)} %copy-done.16, f32[1,2048]{1,0:T(1,128)S(1)} %bitcast.18), custom_call_target="tpu_custom_call" | custom-call | flops 268435456 | bytes 9437184 | tf_op jit(solution)/shard_map/sums/pallas_call | solution.py:354
  54.8 2.0 %collective-permute-start = (f32[8,512]{1,0:T(8,128)S(1)}, f32[8,512]{1,0:T(8,128)S(1)}, u32[]{:S(2)}, u32[]{:S(2)}) collective-permute-start(f32[8,512]{1,0:T(8,128)S(1)} %sums.1.mine), channel_id=1, source_target_pairs={{0,1},{1,0},{2,3},{3,2},{4,5},{5,4},{6,7},{7,6},{8,9},{9,8},{10,11... | collective-permute-start | bytes 49160 | tf_op jit(solution)/shard_map/ppermute | solution.py:304
  56.8 1.8 %collective-permute-done.other = f32[8,512]{1,0:T(8,128)S(1)} collective-permute-done((f32[8,512]{1,0:T(8,128)S(1)}, f32[8,512]{1,0:T(8,128)S(1)}, u32[]{:S(2)}, u32[]{:S(2)}) %collective-permute-start) | collective-permute-done | bytes 16416 | tf_op jit(solution)/shard_map/ppermute | solution.py:304
  58.6 5.8 %norm.1 = (bf16[1,512,2048]{2,1,0:T(8,128)(2,1)}, bf16[512,2048]{1,0:T(8,128)(2,1)S(1)}, bf16[3072,128]{1,0:T(8,128)(2,1)S(1)}) custom-call(s32[1,16]{1,0:T(1,128)S(1)} %copy-done.29, f32[8,512]{1,0:T(8,128)S(1)} %sums.1.mine, f32[8,512]{1,0:T(8,128)S(1)} %collective-permute-done.other, f32[512,2048]{1,0:T(8,128)S(1)} %copy-done.11, ...), custom_call_target="tpu_custom_call" | custom-call | flops 536870912 | bytes 13631488 | tf_op jit(solution)/shard_map/norm/pallas_call | solution.py:364
  66.6 6.4 %all-to-all-start.2 = ((bf16[32,96,128]{2,1,0:T(8,128)(2,1)}), bf16[32,96,128]{2,1,0:T(8,128)(2,1)S(1)}, u32[]{:S(2)}, u32[]{:S(2)}) async-start(bf16[32,96,128]{2,1,0:T(8,128)(2,1)} %bitcast.16), calls=%async_computation.2 | async-start | bytes 1572864 | tf_op jit(solution)/shard_map/all_to_all | solution.py:308
  74.6 1.6 %copy-done.21 = bf16[512,2048]{1,0:T(8,128)(2,1)S(1)} copy-done((bf16[512,2048]{1,0:T(8,128)(2,1)S(1)}, bf16[512,2048]{1,0:T(8,128)(2,1)}, u32[]{:S(2)}) %copy-start.21) | copy-done | bytes 2097176
  77.2 7.7 %grad_query.1 = bf16[1,512,2048]{2,1,0:T(8,128)(2,1)} custom-call(s32[1,16]{1,0:T(1,128)S(1)} %copy-done.29, bf16[512,2048]{1,0:T(8,128)(2,1)S(1)} %copy-done.21, bf16[1,512,2048]{2,1,0:T(8,128)(2,1)S(1)} %copy-done.1, bf16[1,512,2048]{2,1,0:T(8,128)(2,1)S(1)} %copy-done.5, bf16[2048,128]{1,0:T(8,128)(2,1)S(1)} %bitcast.12, bf16[512,512]{1,0:T(8,128)(2,1)S(1)} %copy-done.24), custom_call_target="tpu_custom_call" | custom-call | flops 2147483648 | bytes 9437184 | tf_op jit(solution)/shard_map/grad_query/pallas_call | solution.py:374
  84.9 2.6 %all-to-all-done.2 = bf16[32,96,128]{2,1,0:T(8,128)(2,1)S(1)} async-done(((bf16[32,96,128]{2,1,0:T(8,128)(2,1)}), bf16[32,96,128]{2,1,0:T(8,128)(2,1)S(1)}, u32[]{:S(2)}, u32[]{:S(2)}) %all-to-all-start.2) | async-done | bytes 786464 | tf_op jit(solution)/shard_map/all_to_all | solution.py:308
  89.1 4.8 %all-to-all-start.3 = ((bf16[32,64,128]{2,1,0:T(8,128)(2,1)}), bf16[32,64,128]{2,1,0:T(8,128)(2,1)S(1)}, u32[]{:S(2)}, u32[]{:S(2)}) async-start(bf16[32,64,128]{2,1,0:T(8,128)(2,1)} %bitcast.17), calls=%async_computation.3 | async-start | bytes 1048576 | tf_op jit(solution)/shard_map/all_to_all | solution.py:308
  93.9 4.2 %collective-permute-start.1 = (f32[16,128]{1,0:T(8,128)S(1)}, f32[16,128]{1,0:T(8,128)S(1)}, u32[]{:S(2)}, u32[]{:S(2)}) collective-permute-start(f32[16,128]{1,0:T(8,128)S(1)} %get-tuple-element.39.gg_mine), channel_id=1, source_target_pairs={{0,64},{64,0},{1,65},{65,1},{2,66},{66,2},{3,67},{67,3},{4,68},{68... | collective-permute-start | bytes 24584 | tf_op jit(solution)/shard_map/ppermute | solution.py:304
  98.0 1.6 %copy-done.6 = bf16[1,512,2048]{2,1,0:T(8,128)(2,1)S(1)} copy-done((bf16[1,512,2048]{2,1,0:T(8,128)(2,1)S(1)}, bf16[1,512,2048]{2,1,0:T(8,128)(2,1)}, u32[]{:S(2)}) %copy-start.6) | copy-done | bytes 2097176
  99.6 1.6 %copy-done.15 = bf16[1,512,2048]{2,1,0:T(8,128)(2,1)S(1)} copy-done((bf16[1,512,2048]{2,1,0:T(8,128)(2,1)S(1)}, bf16[1,512,2048]{2,1,0:T(8,128)(2,1)}, u32[]{:S(2)}) %copy-start.15) | copy-done | bytes 2097176
  101.2 1.6 %copy-done.22 = bf16[512,2048]{1,0:T(8,128)(2,1)S(1)} copy-done((bf16[512,2048]{1,0:T(8,128)(2,1)S(1)}, bf16[512,2048]{1,0:T(8,128)(2,1)}, u32[]{:S(2)}) %copy-start.22) | copy-done | bytes 2097176
  103.8 11.5 %grad_local.1 = (f32[512,2048]{1,0:T(8,128)S(1)}, f32[512,2048]{1,0:T(8,128)}) custom-call(bf16[1,512,2048]{2,1,0:T(8,128)(2,1)S(1)} %copy-done.15, bf16[1,512,2048]{2,1,0:T(8,128)(2,1)S(1)} %copy-done.1, bf16[1,512,2048]{2,1,0:T(8,128)(2,1)S(1)} %copy-done.6, bf16[512,2048]{1,0:T(8,128)(2,1)S(1)} %copy-done.22, bf16[512,512]{1,0:T(8,128)(2,1)S(1)} %copy-done.31), custom_call_target="tpu_custom_call" | custom-call | flops 4294967296 | bytes 16777216 | tf_op jit(solution)/shard_map/grad_local/pallas_call | solution.py:391
  115.3 2.0 %copy-done.17 = f32[512,2048]{1,0:T(8,128)} copy-done((f32[512,2048]{1,0:T(8,128)}, f32[512,2048]{1,0:T(8,128)S(1)}, u32[]{:S(2)}) %copy-start.17) | copy-done | bytes 4194328
  118.9 2.2 %copy-done.18 = f32[512,2048]{1,0:T(8,128)S(1)} copy-done((f32[512,2048]{1,0:T(8,128)S(1)}, f32[512,2048]{1,0:T(8,128)}, u32[]{:S(2)}) %copy-start.18) | copy-done | bytes 4194328
  121.1 2.2 %copy-done.19 = f32[512,2048]{1,0:T(8,128)S(1)} copy-done((f32[512,2048]{1,0:T(8,128)S(1)}, f32[512,2048]{1,0:T(8,128)}, u32[]{:S(2)}) %copy-start.19) | copy-done | bytes 4194328
  123.3 4.4 %grad_close.1 = (bf16[1,512,2048]{2,1,0:T(8,128)(2,1)}, bf16[1,512,2048]{2,1,0:T(8,128)(2,1)}, f32[16,128]{1,0:T(8,128)}) custom-call(s32[1,16]{1,0:T(1,128)S(1)} %copy-done.29, f32[512,2048]{1,0:T(8,128)S(1)} %copy-done.18, f32[512,2048]{1,0:T(8,128)S(1)} %copy-done.19, bf16[1,512,2048]{2,1,0:T(8,128)(2,1)S(1)} %copy-done.1, ...), custom_call_target="tpu_custom_call" | custom-call | flops 536870912 | bytes 17825792 | tf_op jit(solution)/shard_map/grad_close/pallas_call | solution.py:399
  (54 shorter events, 18.6 us)
Async XLA Ops:
  0.6 1.6 %copy-start = (bf16[1,512,2048]{2,1,0:T(8,128)(2,1)S(1)}, bf16[1,512,2048]{2,1,0:T(8,128)(2,1)}, u32[]{:S(2)}) copy-start(bf16[1,512,2048]{2,1,0:T(8,128)(2,1)} %k.11) | copy-start | bytes 6291460
  2.2 1.6 %copy-start.2 = (bf16[1,512,2048]{2,1,0:T(8,128)(2,1)S(1)}, bf16[1,512,2048]{2,1,0:T(8,128)(2,1)}, u32[]{:S(2)}) copy-start(bf16[1,512,2048]{2,1,0:T(8,128)(2,1)} %v.11) | copy-start | bytes 6291460
  4.5 10.7 %copy-start.1 = (bf16[1,512,2048]{2,1,0:T(8,128)(2,1)S(1)}, bf16[1,512,2048]{2,1,0:T(8,128)(2,1)}, u32[]{:S(2)}) copy-start(bf16[1,512,2048]{2,1,0:T(8,128)(2,1)} %k.11) | copy-start | bytes 6291460
  4.5 10.7 %copy-start.29 = (s32[1,16]{1,0:T(1,128)S(1)}, s32[1,16]{1,0:T(1,128)}, u32[]{:S(2)}) copy-start(s32[1,16]{1,0:T(1,128)} %lens.15) | copy-start | bytes 196
  7.7 19.0 %all-to-all-start = ((bf16[32,64,128]{2,1,0:T(8,128)(2,1)}), bf16[32,64,128]{2,1,0:T(8,128)(2,1)S(1)}, u32[]{:S(2)}, u32[]{:S(2)}) async-start(bf16[32,64,128]{2,1,0:T(8,128)(2,1)} %bitcast), calls=%async_computation | async-start | bytes 1048576 | tf_op jit(solution)/shard_map/all_to_all | solution.py:308
  15.1 1.6 %copy-start.3 = (bf16[1,512,2048]{2,1,0:T(8,128)(2,1)S(1)}, bf16[1,512,2048]{2,1,0:T(8,128)(2,1)}, u32[]{:S(2)}) copy-start(bf16[1,512,2048]{2,1,0:T(8,128)(2,1)} %v.11) | copy-start | bytes 6291460
  16.7 1.6 %copy-start.12 = (bf16[1,512,2048]{2,1,0:T(8,128)(2,1)S(1)}, bf16[1,512,2048]{2,1,0:T(8,128)(2,1)}, u32[]{:S(2)}) copy-start(bf16[1,512,2048]{2,1,0:T(8,128)(2,1)} %q.9) | copy-start | bytes 6291460
  23.1 2.0 %copy-start.8 = (f32[512,2048]{1,0:T(8,128)}, f32[512,2048]{1,0:T(8,128)S(1)}, u32[]{:S(2)}) copy-start(f32[512,2048]{1,0:T(8,128)S(1)} %get-tuple-element.26.unused) | copy-start | bytes 12582916
  25.8 17.5 %copy-start.23 = (bf16[512,512]{1,0:T(8,128)(2,1)}, bf16[512,512]{1,0:T(8,128)(2,1)S(1)}, u32[]{:S(2)}) copy-start(bf16[512,512]{1,0:T(8,128)(2,1)S(1)} %get-tuple-element.24.mask) | copy-start | bytes 1572868
  28.2 18.1 %all-to-all-start.1 = ((bf16[32,64,128]{2,1,0:T(8,128)(2,1)}), bf16[32,64,128]{2,1,0:T(8,128)(2,1)S(1)}, u32[]{:S(2)}, u32[]{:S(2)}) async-start(bf16[32,64,128]{2,1,0:T(8,128)(2,1)} %bitcast.2), calls=%async_computation.1 | async-start | bytes 1048576 | tf_op jit(solution)/shard_map/all_to_all | solution.py:308
  34.7 1.6 %copy-start.4 = (bf16[1,512,2048]{2,1,0:T(8,128)(2,1)S(1)}, bf16[1,512,2048]{2,1,0:T(8,128)(2,1)}, u32[]{:S(2)}) copy-start(bf16[1,512,2048]{2,1,0:T(8,128)(2,1)} %v.11) | copy-start | bytes 6291460
  36.3 2.2 %copy-start.9 = (f32[512,2048]{1,0:T(8,128)S(1)}, f32[512,2048]{1,0:T(8,128)}, u32[]{:S(2)}) copy-start(f32[512,2048]{1,0:T(8,128)} %copy-done.8) | copy-start | bytes 12582916
  38.5 1.6 %copy-start.13 = (bf16[1,512,2048]{2,1,0:T(8,128)(2,1)S(1)}, bf16[1,512,2048]{2,1,0:T(8,128)(2,1)}, u32[]{:S(2)}) copy-start(bf16[1,512,2048]{2,1,0:T(8,128)(2,1)} %q.9) | copy-start | bytes 6291460
  40.1 6.2 %copy-start.27 = (f32[2048]{0:T(1024)S(1)}, f32[2048]{0:T(1024)}, u32[]{:S(2)}) copy-start(f32[2048]{0:T(1024)} %param.11) | copy-start | bytes 24580
  43.4 2.0 %copy-start.10 = (f32[512,2048]{1,0:T(8,128)}, f32[512,2048]{1,0:T(8,128)S(1)}, u32[]{:S(2)}) copy-start(f32[512,2048]{1,0:T(8,128)S(1)} %attend_second.1.local) | copy-start | bytes 12582916
  46.3 2.2 %copy-start.11 = (f32[512,2048]{1,0:T(8,128)S(1)}, f32[512,2048]{1,0:T(8,128)}, u32[]{:S(2)}) copy-start(f32[512,2048]{1,0:T(8,128)} %copy-done.10) | copy-start | bytes 12582916
  48.5 1.6 %copy-start.14 = (bf16[1,512,2048]{2,1,0:T(8,128)(2,1)S(1)}, bf16[1,512,2048]{2,1,0:T(8,128)(2,1)}, u32[]{:S(2)}) copy-start(bf16[1,512,2048]{2,1,0:T(8,128)(2,1)} %q.9) | copy-start | bytes 6291460
  50.1 1.6 %copy-start.16 = (bf16[1,512,2048]{2,1,0:T(8,128)(2,1)S(1)}, bf16[1,512,2048]{2,1,0:T(8,128)(2,1)}, u32[]{:S(2)}) copy-start(bf16[1,512,2048]{2,1,0:T(8,128)(2,1)} %up.3) | copy-start | bytes 6291460
  54.8 3.8 %collective-permute-start = (f32[8,512]{1,0:T(8,128)S(1)}, f32[8,512]{1,0:T(8,128)S(1)}, u32[]{:S(2)}, u32[]{:S(2)}) collective-permute-start(f32[8,512]{1,0:T(8,128)S(1)} %sums.1.mine), channel_id=1, source_target_pairs={{0,1},{1,0},{2,3},{3,2},{4,5},{5,4},{6,7},{7,6},{8,9},{9,8},{10,11... | collective-permute-start | bytes 49160 | tf_op jit(solution)/shard_map/ppermute | solution.py:304
  64.4 1.3 %copy-start.20 = (bf16[512,2048]{1,0:T(8,128)(2,1)}, bf16[512,2048]{1,0:T(8,128)(2,1)S(1)}, u32[]{:S(2)}) copy-start(bf16[512,2048]{1,0:T(8,128)(2,1)S(1)} %get-tuple-element.34.d_att) | copy-start | bytes 6291460
  66.6 20.9 %all-to-all-start.2 = ((bf16[32,96,128]{2,1,0:T(8,128)(2,1)}), bf16[32,96,128]{2,1,0:T(8,128)(2,1)S(1)}, u32[]{:S(2)}, u32[]{:S(2)}) async-start(bf16[32,96,128]{2,1,0:T(8,128)(2,1)} %bitcast.16), calls=%async_computation.2 | async-start | bytes 1572864 | tf_op jit(solution)/shard_map/all_to_all | solution.py:308
  73.0 1.6 %copy-start.5 = (bf16[1,512,2048]{2,1,0:T(8,128)(2,1)S(1)}, bf16[1,512,2048]{2,1,0:T(8,128)(2,1)}, u32[]{:S(2)}) copy-start(bf16[1,512,2048]{2,1,0:T(8,128)(2,1)} %v.11) | copy-start | bytes 6291460
  74.6 1.6 %copy-start.21 = (bf16[512,2048]{1,0:T(8,128)(2,1)S(1)}, bf16[512,2048]{1,0:T(8,128)(2,1)}, u32[]{:S(2)}) copy-start(bf16[512,2048]{1,0:T(8,128)(2,1)} %copy-done.20) | copy-start | bytes 6291460
  89.1 28.3 %all-to-all-start.3 = ((bf16[32,64,128]{2,1,0:T(8,128)(2,1)}), bf16[32,64,128]{2,1,0:T(8,128)(2,1)S(1)}, u32[]{:S(2)}, u32[]{:S(2)}) async-start(bf16[32,64,128]{2,1,0:T(8,128)(2,1)} %bitcast.17), calls=%async_computation.3 | async-start | bytes 1048576 | tf_op jit(solution)/shard_map/all_to_all | solution.py:308
  93.9 23.5 %collective-permute-start.1 = (f32[16,128]{1,0:T(8,128)S(1)}, f32[16,128]{1,0:T(8,128)S(1)}, u32[]{:S(2)}, u32[]{:S(2)}) collective-permute-start(f32[16,128]{1,0:T(8,128)S(1)} %get-tuple-element.39.gg_mine), channel_id=1, source_target_pairs={{0,64},{64,0},{1,65},{65,1},{2,66},{66,2},{3,67},{67,3},{4,68},{68... | collective-permute-start | bytes 24584 | tf_op jit(solution)/shard_map/ppermute | solution.py:304
  98.0 1.6 %copy-start.6 = (bf16[1,512,2048]{2,1,0:T(8,128)(2,1)S(1)}, bf16[1,512,2048]{2,1,0:T(8,128)(2,1)}, u32[]{:S(2)}) copy-start(bf16[1,512,2048]{2,1,0:T(8,128)(2,1)} %v.11) | copy-start | bytes 6291460
  99.6 1.6 %copy-start.15 = (bf16[1,512,2048]{2,1,0:T(8,128)(2,1)S(1)}, bf16[1,512,2048]{2,1,0:T(8,128)(2,1)}, u32[]{:S(2)}) copy-start(bf16[1,512,2048]{2,1,0:T(8,128)(2,1)} %q.9) | copy-start | bytes 6291460
  101.2 1.6 %copy-start.22 = (bf16[512,2048]{1,0:T(8,128)(2,1)S(1)}, bf16[512,2048]{1,0:T(8,128)(2,1)}, u32[]{:S(2)}) copy-start(bf16[512,2048]{1,0:T(8,128)(2,1)} %copy-done.20) | copy-start | bytes 6291460
  115.3 2.0 %copy-start.17 = (f32[512,2048]{1,0:T(8,128)}, f32[512,2048]{1,0:T(8,128)S(1)}, u32[]{:S(2)}) copy-start(f32[512,2048]{1,0:T(8,128)S(1)} %get-tuple-element.36.gk_local) | copy-start | bytes 12582916
  117.3 1.6 %copy-start.7 = (bf16[1,512,2048]{2,1,0:T(8,128)(2,1)S(1)}, bf16[1,512,2048]{2,1,0:T(8,128)(2,1)}, u32[]{:S(2)}) copy-start(bf16[1,512,2048]{2,1,0:T(8,128)(2,1)} %v.11) | copy-start | bytes 6291460
  118.9 2.2 %copy-start.18 = (f32[512,2048]{1,0:T(8,128)S(1)}, f32[512,2048]{1,0:T(8,128)}, u32[]{:S(2)}) copy-start(f32[512,2048]{1,0:T(8,128)} %copy-done.17) | copy-start | bytes 12582916
  121.1 2.2 %copy-start.19 = (f32[512,2048]{1,0:T(8,128)S(1)}, f32[512,2048]{1,0:T(8,128)}, u32[]{:S(2)}) copy-start(f32[512,2048]{1,0:T(8,128)} %get-tuple-element.37.gv_local) | copy-start | bytes 12582916
  (6 other events, 5.2 us)

commit v2 on v0

v2 whole, which is shorter than its diff:
```python
import jax
import jax.numpy as jnp
from jax import lax
from jax.experimental import pallas as pl
from jax.experimental.pallas import tpu as pltpu
from jax.sharding import PartitionSpec as P

HEADS = 32
HD = 128
TOK = 512
HALF = 256
N_SEQ = 32
SLICE = 64
GG_ROWS = 32
GROUP = 2
EPS = 1e-05
BACK_SPLIT = 10

F32 = jnp.float32
BF16 = jnp.bfloat16
LOCAL = BF16
NN = (((1,), (0,)), ((), ()))
NT = (((1,), (1,)), ((), ()))
TN = (((0,), (0,)), ((), ()))
HALVES = (slice(0, HALF), slice(HALF, TOK))


def mm(a, b, dims):
    return lax.dot_general(a, b, dims, preferred_element_type=F32)


def cols(g):
    return slice(g * HD, (g + 1) * HD)


def local_starts(lens):
    total = -(lax.axis_index("seq") * TOK)
    starts = []
    for d in range(lens.shape[1]):
        starts.append(total)
        total = total + lens[0, d]
    return starts


def front_end(starts, begin, end):
    stop = jnp.int32(end)
    fresh = jnp.int32(0)
    for s in reversed(starts):
        stop = jnp.where(s > begin, s, stop)
        fresh = jnp.where(s == begin, 1, fresh)
    return jnp.where(fresh == 1, begin, jnp.minimum(stop, end))


def tail_start(starts, begin, end):
    start = jnp.int32(begin)
    for s in starts:
        start = jnp.where(s < end, s, start)
    return jnp.maximum(start, begin)


def keep_of(starts, begin, end):
    hit = jnp.int32(0)
    for s in starts:
        hit = jnp.where((s >= begin) & (s < end), 1, hit)
    return (1 - hit).astype(F32)


def front_mask(starts):
    t = lax.broadcasted_iota(jnp.int32, (TOK, HD), 0)
    limit = jnp.where(t < HALF, front_end(starts, 0, HALF), front_end(starts, HALF, TOK))
    return jnp.where(t < limit, 1.0, 0.0).astype(BF16)


def tail_mask(starts):
    t = lax.broadcasted_iota(jnp.int32, (TOK, HD), 0)
    limit = jnp.where(t < HALF, tail_start(starts, 0, HALF), tail_start(starts, HALF, TOK))
    return jnp.where(t >= limit, 1.0, 0.0).astype(BF16)


def keeps(lens):
    bits = jnp.int32(0)
    total = jnp.int32(0)
    for d in range(lens.shape[1]):
        bits = bits | lax.shift_left(jnp.int32(1), lax.shift_right_logical(total, 9))
        total = total + lens[0, d]
    return [(1 - (lax.shift_right_logical(bits, b) & 1)).astype(F32) for b in range(N_SEQ)]


def build_masks(starts, mask, mask_t):
    t = lax.broadcasted_iota(jnp.int32, (TOK, HD), 0)
    lane = lax.broadcasted_iota(jnp.int32, (TOK, HD), 1)
    base = jnp.where(t < HALF, lane, lane + HALF)
    begin = jnp.zeros((TOK, HD), jnp.int32)
    for s in starts:
        begin = jnp.where(t >= s, jnp.maximum(s, 0), begin)
    end = jnp.full((TOK, HD), TOK, jnp.int32)
    for s in reversed(starts):
        end = jnp.where(s > t, jnp.minimum(s, TOK), end)
    for c in range(HALF // HD):
        s = base + c * HD
        mask[:, cols(c)] = jnp.where((s <= t) & (s >= begin), 1.0, 0.0).astype(BF16)
        mask_t[:, cols(c)] = jnp.where((s >= t) & (s < end), 1.0, 0.0).astype(BF16)


def second_carry(own, keep, earlier):
    return (own.astype(F32) + keep * earlier.astype(F32)).astype(BF16)


def token_cols(ref, h):
    return ref.at[0, :, pl.ds(h * HD if isinstance(h, int) else pl.multiple_of(h * HD, HD), HD)]


def head_rows(ref, h):
    return ref.at[pl.ds(h * HD if isinstance(h, int) else pl.multiple_of(h * HD, HD), HD), :]


def chunk(ref, h):
    return ref.at[h]


class Stream:
    def __init__(self, hbm, view, buf, sem, first=0, out=False):
        self.hbm, self.view, self.buf, self.sem, self.first, self.out = hbm, view, buf, sem, first, out

    def copy(self, i):
        far, near = self.view(self.hbm, i + self.first), self.buf.at[i]
        src, dst = (near, far) if self.out else (far, near)
        return pltpu.make_async_copy(src, dst, self.sem.at[i])

    def start(self, i):
        self.copy(i).start()

    def wait(self, i):
        self.copy(i).wait()


def start_all(n, streams):
    for i in range(n):
        for s in streams:
            s.start(i)


def loop(n, ins, outs, step, group=GROUP):
    def one(j, carry):
        for g in range(group):
            for s in ins:
                s.wait(j * group + g)
        for g in range(group):
            step(j * group + g)
        for g in range(group):
            for s in outs:
                s.start(j * group + g)
        return carry

    lax.fori_loop(0, n // group, one, 0)
    for i in range(n):
        for s in outs:
            s.wait(i)


def state_kernel(lens, k, v, out, early, k_buf, v_buf, o_buf, e_buf, mask, lens_s, lens_sem, sems):
    n = k_buf.shape[0]
    ahead = pltpu.make_async_copy(lens, lens_s, lens_sem)
    ahead.start()
    ins = [Stream(k, token_cols, k_buf, sems.at[0]), Stream(v, token_cols, v_buf, sems.at[1])]
    start_all(n, ins)
    ahead.wait()
    starts = local_starts(lens_s)
    mask[...] = tail_mask(starts)
    keep = keep_of(starts, HALF, TOK)

    def step(i):
        a, b = (mm(k_buf[i, r, :] * mask[r, :], v_buf[i, r, :], TN) for r in HALVES)
        e_buf[i] = a.astype(BF16)
        o_buf[i] = (b + keep * a).astype(BF16)

    loop(n, ins, [Stream(out, head_rows, o_buf, sems.at[2], out=True),
                  Stream(early, head_rows, e_buf, sems.at[3], out=True)], step)


def scan_kernel(lens, x, out, x_buf, o_buf, lens_s, lens_sem, sems):
    n = x_buf.shape[0]
    rows = x_buf.shape[2]
    view = lambda ref, i: ref.at[:, pl.ds(i * rows, rows), :]
    ahead = pltpu.make_async_copy(lens, lens_s, lens_sem)
    ahead.start()
    ins = [Stream(x, view, x_buf, sems.at[0])]
    start_all(n, ins)
    ahead.wait()
    keep = keeps(lens_s)

    def step(i):
        acc = jnp.zeros((rows, HD), F32)
        for b in range(N_SEQ):
            o_buf[i, b] = acc.astype(BF16)
            acc = x_buf[i, b].astype(F32) + keep[b] * acc

    loop(n, ins, [Stream(out, view, o_buf, sems.at[1], out=True)], step, group=1)


def scan_back_kernel(lens, x, out, gg, x_buf, o_buf, g_buf, lens_s, lens_sem, sems):
    n = x_buf.shape[0]
    rows = x_buf.shape[2]
    view = lambda ref, i: ref.at[:, pl.ds(i * rows, rows), :]
    ahead = pltpu.make_async_copy(lens, lens_s, lens_sem)
    ahead.start()
    ins = [Stream(x, view, x_buf, sems.at[0])]
    start_all(n, ins)
    gains = pltpu.make_async_copy(x.at[:, pl.ds(SLICE, GG_ROWS), :], g_buf, sems.at[2, 0])
    gains.start()
    ahead.wait()
    keep = keeps(lens_s)

    def step(i):
        acc = jnp.zeros((rows, HD), F32)
        for b in reversed(range(N_SEQ)):
            o_buf[i, b] = acc.astype(BF16)
            acc = x_buf[i, b].astype(F32) + keep[b] * acc

    loop(n, ins, [Stream(out, view, o_buf, sems.at[1], out=True)], step, group=1)
    gains.wait()
    half = GG_ROWS // 2
    total = jnp.zeros((half, HD), F32)
    for b in range(N_SEQ):
        total = total + (g_buf[b, 0:half, :].astype(F32) + g_buf[b, half:GG_ROWS, :].astype(F32))
    gg[...] = total


def attend_head(q, k, v, mask, out, i):
    for r in HALVES:
        s = mm(q[i, r, :], k[i, r, :], NT).astype(BF16) * mask[r, :]
        out[i, r, :] = mm(s, v[i, r, :], NN).astype(LOCAL)


def attend_first_kernel(lens, q, k, v, out, mask_out, mask_t_out, q_buf, k_buf, v_buf, o_buf,
                        mask, mask_t, lens_s, lens_sem, mask_sem, sems):
    n = q_buf.shape[0]
    ahead = pltpu.make_async_copy(lens, lens_s, lens_sem)
    ahead.start()
    ins = [Stream(ref, token_cols, buf, sems.at[j])
           for j, (ref, buf) in enumerate(((q, q_buf), (k, k_buf), (v, v_buf)))]
    start_all(n, ins)
    ahead.wait()
    build_masks(local_starts(lens_s), mask, mask_t)
    one = pltpu.make_async_copy(mask, mask_out, mask_sem.at[0])
    two = pltpu.make_async_copy(mask_t, mask_t_out, mask_sem.at[1])
    one.start()
    two.start()
    loop(n, ins, [Stream(out, chunk, o_buf, sems.at[3], out=True)],
         lambda i: attend_head(q_buf, k_buf, v_buf, mask, o_buf, i))
    one.wait()
    two.wait()


def attend_second_kernel(q, k, v, mask_in, unused, out, q_buf, k_buf, v_buf, o_buf,
                         mask, mask_sem, sems):
    n = q_buf.shape[0]
    first = out.shape[0] - n
    ahead = pltpu.make_async_copy(mask_in, mask, mask_sem)
    ahead.start()
    ins = [Stream(ref, token_cols, buf, sems.at[j], first=first)
           for j, (ref, buf) in enumerate(((q, q_buf), (k, k_buf), (v, v_buf)))]
    start_all(n, ins)
    ahead.wait()
    loop(n, ins, [Stream(out, chunk, o_buf, sems.at[3], first=first, out=True)],
         lambda i: attend_head(q_buf, k_buf, v_buf, mask, o_buf, i))


def sums_kernel(lens, local, q, carry, early, up, gain, out, local_buf, q_buf, carry_buf, early_buf,
                up_buf, gain_buf, mask, squares, inners, lens_s, lens_sem, sems):
    n = q_buf.shape[0]
    ahead = pltpu.make_async_copy(lens, lens_s, lens_sem)
    ahead.start()
    scales = pltpu.make_async_copy(gain, gain_buf, sems.at[5, 0])
    scales.start()
    ins = [Stream(local, chunk, local_buf, sems.at[0]),
           Stream(q, token_cols, q_buf, sems.at[1]),
           Stream(carry, head_rows, carry_buf, sems.at[2]),
           Stream(early, head_rows, early_buf, sems.at[3]),
           Stream(up, token_cols, up_buf, sems.at[4])]
    start_all(n, ins)
    ahead.wait()
    starts = local_starts(lens_s)
    mask[...] = front_mask(starts)
    keep = keep_of(starts, 0, HALF)
    squares[...] = jnp.zeros((TOK, HD), F32)
    inners[...] = jnp.zeros((TOK, HD), F32)
    scales.wait()

    def step(i):
        carries = (carry_buf[i], second_carry(early_buf[i], keep, carry_buf[i]))
        for r, c in zip(HALVES, carries):
            a = local_buf[i, r, :].astype(F32) + mm(q_buf[i, r, :] * mask[r, :], c, NN)
            squares[r, :] = squares[r, :] + a * a
            inners[r, :] = inners[r, :] + a * (up_buf[i, r, :].astype(F32) * gain_buf[i])

    loop(n, ins, [], step)
    ones = jnp.ones((8, HD), F32)
    row = lax.broadcasted_iota(jnp.int32, (8, TOK), 0)
    exact = dict(precision=lax.Precision.HIGHEST, preferred_element_type=F32)
    one = lax.dot_general(ones, squares[...], NT, **exact)
    two = lax.dot_general(ones, inners[...], NT, **exact)
    out[...] = jnp.where(row == 0, one, two)


def norm_kernel(lens, mine, other, local, q, carry, early, up, gain, layer, d_att, send, late,
                local_buf, q_buf, carry_buf, early_buf, up_buf, layer_buf, d_buf, send_buf, late_buf, mask, rscale, inner, gains,
                lens_s, lens_sem, sems):
    n = q_buf.shape[0]
    ahead = pltpu.make_async_copy(lens, lens_s, lens_sem)
    ahead.start()
    ins = [Stream(local, chunk, local_buf, sems.at[0]),
           Stream(q, token_cols, q_buf, sems.at[1]),
           Stream(carry, head_rows, carry_buf, sems.at[2]),
           Stream(early, head_rows, early_buf, sems.at[3]),
           Stream(up, token_cols, up_buf, sems.at[4])]
    start_all(n, ins)
    both = jnp.transpose(mine[...] + other[...], (1, 0))
    scale = 1.0 / (HEADS * HD)
    rs = lax.rsqrt(jnp.broadcast_to(both[:, 0:1], (TOK, HD)) * scale + EPS)
    rscale[...] = rs
    inner[...] = rs * (jnp.broadcast_to(both[:, 1:2], (TOK, HD)) * scale)
    ahead.wait()
    starts = local_starts(lens_s)
    mask[...] = front_mask(starts)
    keep = keep_of(starts, 0, HALF)

    def step(i):
        gg = gain[i]
        total = jnp.zeros((1, HD), F32)
        backs = []
        carries = (carry_buf[i], second_carry(early_buf[i], keep, carry_buf[i]))
        for r, c in zip(HALVES, carries):
            rs = rscale[r, :]
            front = q_buf[i, r, :] * mask[r, :]
            unit = (local_buf[i, r, :].astype(F32) + mm(front, c, NN)) * rs
            layer_buf[i, r, :] = (gg * unit).astype(BF16)
            upstream = up_buf[i, r, :].astype(F32)
            total = total + jnp.sum(upstream * unit, axis=0, keepdims=True)
            da = (rs * (upstream * gg - unit * inner[r, :])).astype(BF16)
            d_buf[i, r, :] = da
            backs.append(mm(front, da, TN))
        gains[pl.ds(i, 1), :] = total
        late_buf[i] = backs[1].astype(BF16)
        back = (backs[0] + keep * backs[1]).astype(BF16)
        send_buf[2 * i, 0:SLICE, :] = back[0:SLICE, :]
        send_buf[2 * i + 1, 0:SLICE, :] = back[SLICE:HD, :]

    loop(n, ins, [Stream(layer, token_cols, layer_buf, sems.at[5], out=True),
                  Stream(d_att, chunk, d_buf, sems.at[6], out=True),
                  Stream(late, head_rows, late_buf, sems.at[7], out=True)], step)
    total = gains[...]
    high = total.astype(BF16)
    low = (total - high.astype(F32)).astype(BF16)
    half = GG_ROWS // 2
    for b in range(N_SEQ):
        send_buf[b, SLICE:SLICE + half, :] = high
        send_buf[b, SLICE + half:SLICE + GG_ROWS, :] = low
    last = pltpu.make_async_copy(send_buf, send, lens_sem)
    last.start()
    last.wait()


def grad_kernel(first, lens, d_att, q, k, v, carry, early, mask_in, mask_t_in, gq, gk, gv,
                d_buf, q_buf, k_buf, v_buf, c_buf, e_buf, gq_buf, gk_buf, gv_buf,
                mask, mask_t, front, lens_s, lens_sem, mask_sem, sems):
    n = q_buf.shape[0]
    ahead = pltpu.make_async_copy(lens, lens_s, lens_sem)
    ahead.start()
    one = pltpu.make_async_copy(mask_in, mask, mask_sem.at[0])
    two = pltpu.make_async_copy(mask_t_in, mask_t, mask_sem.at[1])
    one.start()
    two.start()
    ins = [Stream(d_att, chunk, d_buf, sems.at[0], first=first),
           Stream(q, token_cols, q_buf, sems.at[1], first=first),
           Stream(k, token_cols, k_buf, sems.at[2], first=first),
           Stream(v, token_cols, v_buf, sems.at[3], first=first),
           Stream(carry, head_rows, c_buf, sems.at[4], first=first),
           Stream(early, head_rows, e_buf, sems.at[5], first=first)]
    start_all(n, ins)
    ahead.wait()
    starts = local_starts(lens_s)
    front[...] = front_mask(starts)
    keep = keep_of(starts, 0, HALF)
    one.wait()
    two.wait()

    def step(i):
        carries = (c_buf[i], second_carry(e_buf[i], keep, c_buf[i]))
        for r, c in zip(HALVES, carries):
            da, qr, kr, vr = d_buf[i, r, :], q_buf[i, r, :], k_buf[i, r, :], v_buf[i, r, :]
            ds = mm(da, vr, NT).astype(BF16) * mask[r, :]
            gq_buf[i, r, :] = (mm(ds, kr, NN) + mm(da * front[r, :], c, NT)).astype(BF16)
            s = mm(kr, qr, NT).astype(BF16) * mask_t[r, :]
            gv_buf[i, r, :] = mm(s, da, NN).astype(LOCAL)
            ds = mm(vr, da, NT).astype(BF16) * mask_t[r, :]
            gk_buf[i, r, :] = mm(ds, qr, NN).astype(LOCAL)

    outs = [Stream(gq, token_cols, gq_buf, sems.at[6], first=first, out=True),
            Stream(gk, chunk, gk_buf, sems.at[7], first=first, out=True),
            Stream(gv, chunk, gv_buf, sems.at[8], first=first, out=True)]
    loop(n, ins, outs, step)


def close_kernel(lens, gk_local, gv_local, k, v, carry, late, gg_mine, gg_other, gk, gv, gg,
                 gk_buf, gv_buf, k_buf, v_buf, c_buf, l_buf, gk_out, gv_out, mask, lens_s, lens_sem, sems):
    n = k_buf.shape[0]
    ahead = pltpu.make_async_copy(lens, lens_s, lens_sem)
    ahead.start()
    ins = [Stream(gk_local, chunk, gk_buf, sems.at[0]),
           Stream(gv_local, chunk, gv_buf, sems.at[1]),
           Stream(k, token_cols, k_buf, sems.at[2]),
           Stream(v, token_cols, v_buf, sems.at[3]),
           Stream(carry, head_rows, c_buf, sems.at[4]),
           Stream(late, head_rows, l_buf, sems.at[5])]
    start_all(n, ins)
    gg[...] = gg_mine[...] + gg_other[...]
    ahead.wait()
    starts = local_starts(lens_s)
    mask[...] = tail_mask(starts)
    keep = keep_of(starts, HALF, TOK)

    def step(i):
        carries = (second_carry(l_buf[i], keep, c_buf[i]), c_buf[i])
        for r, c in zip(HALVES, carries):
            m = mask[r, :]
            gk_out[i, r, :] = (gk_buf[i, r, :].astype(F32) + mm(v_buf[i, r, :] * m, c, NT)).astype(BF16)
            gv_out[i, r, :] = (gv_buf[i, r, :].astype(F32) + mm(k_buf[i, r, :] * m, c, NN)).astype(BF16)

    loop(n, ins, [Stream(gk, token_cols, gk_out, sems.at[6], out=True),
                  Stream(gv, token_cols, gv_out, sems.at[7], out=True)], step)


HBM = pl.BlockSpec(memory_space=pltpu.HBM)
ANY = pl.BlockSpec(memory_space=pl.ANY)
NEAR = pl.BlockSpec(memory_space=pltpu.VMEM)
MB = 1 << 20
FULL_GRANT = 60 * MB
PART_GRANT = 52 * MB
SMALL_GRANT = 8 * MB
SCALARS = [pltpu.SMEM((1, 16), jnp.int32), pltpu.SemaphoreType.DMA(())]


def struct(shape, dtype):
    return jax.ShapeDtypeStruct(shape, dtype)


def near(shape, dtype):
    return pltpu.VMEM(shape, dtype)


def call(kernel, name, ins, outs, out_shape, scratch, flops, traffic, grant=FULL_GRANT, alias=None):
    return pl.pallas_call(
        kernel, name=name, in_specs=ins, out_specs=outs, out_shape=out_shape,
        scratch_shapes=scratch, input_output_aliases=alias or {},
        compiler_params=pltpu.CompilerParams(vmem_limit_bytes=grant),
        cost_estimate=pl.CostEstimate(flops=flops, transcendentals=0, bytes_accessed=traffic))


def sems(*shape):
    return pltpu.SemaphoreType.DMA(shape)


def exchange(x, axis):
    return lax.ppermute(x, axis, [(0, 1), (1, 0)])


def swap(x):
    return lax.all_to_all(x, "seq", 0, 0, tiled=True)


def body(queries, keys, values, grad_out, lens, gain):
    width = queries.shape[2]
    n = width // HD
    half = n // 2
    gain = gain.reshape(n, 1, HD)
    unit = 2 * n * TOK * TOK * HD
    wide = struct((1, TOK, width), BF16)
    state_shape = (n * HD, HD)
    head_shape = (n, TOK, HD)
    slices = (N_SEQ, SLICE, HD)
    tok = lambda m, dtype=BF16: near((m, TOK, HD), dtype)
    sq = lambda m: near((m, HD, HD), BF16)
    column = lambda dtype: near((TOK, HD), dtype)
    square = near((TOK, HALF), BF16)
    mask_shape = struct((TOK, HALF), BF16)
    parts = 4
    scan_buf = near((parts, N_SEQ, SLICE // parts, HD), BF16)

    state, early = call(
        state_kernel, "state", [HBM] * 3, [HBM] * 2, [struct(state_shape, BF16)] * 2,
        [tok(n), tok(n), sq(n), sq(n), column(BF16)] + SCALARS + [sems(4, n)], unit // 4, 5 * MB,
    )(lens, keys, values)
    scattered = swap(state)
    local, mask, mask_t = call(
        attend_first_kernel, "attend_first", [HBM] * 4, [HBM] * 3,
        [struct(head_shape, LOCAL), mask_shape, mask_shape],
        [tok(half), tok(half), tok(half), tok(half, LOCAL), square, square] + SCALARS
        + [sems(2), sems(4, half)], unit, 6 * MB,
    )(lens, queries, keys, values)
    summed = call(
        scan_kernel, "scan", [ANY] * 2, ANY, struct(slices, BF16),
        [scan_buf, scan_buf] + SCALARS + [sems(2, parts)], MB, MB, grant=SMALL_GRANT,
    )(lens, scattered.reshape(slices))
    summed, local = lax.optimization_barrier((summed, local))
    carry_in = swap(summed).reshape(state_shape)
    local = call(
        attend_second_kernel, "attend_second", [HBM] * 5, HBM, struct(head_shape, LOCAL),
        [tok(half), tok(half), tok(half), tok(half, LOCAL), square, sems(), sems(4, half)],
        unit, 6 * MB, alias={4: 0},
    )(queries, keys, values, mask, local)
    sums = call(
        sums_kernel, "sums", [ANY] * 7, NEAR, struct((8, TOK), F32),
        [tok(n, LOCAL), tok(n), sq(n), sq(n), tok(n), near((n, 1, HD), F32), column(BF16),
         column(F32), column(F32)] + SCALARS + [sems(6, n)], unit // 4, 9 * MB, grant=PART_GRANT,
    )(lens, local, queries, carry_in, early, grad_out, gain)
    other = exchange(sums, "tensor")
    send_shape = (N_SEQ, SLICE + GG_ROWS, HD)
    layer_out, d_att, send, late = call(
        norm_kernel, "norm", [ANY] + [NEAR] * 2 + [ANY] * 5 + [NEAR], [ANY] * 4,
        [wide, struct(head_shape, BF16), struct(send_shape, BF16), struct(state_shape, BF16)],
        [tok(n, LOCAL), tok(n), sq(n), sq(n), tok(n), tok(n), tok(n), near(send_shape, BF16), sq(n),
         column(BF16), column(F32), column(F32), near((n, HD), F32)] + SCALARS + [sems(8, n)],
        unit // 2, 13 * MB, grant=PART_GRANT,
    )(lens, sums, other, local, queries, carry_in, early, grad_out, gain)
    back = swap(send)

    def gradients(first, count, *earlier):
        def kernel(*refs):
            grad_kernel(first, *refs[:9], *refs[9 + len(earlier):])

        return call(
            kernel, f"grad_from_{first}", [HBM] * (9 + len(earlier)), [HBM] * 3,
            [wide, struct(head_shape, LOCAL), struct(head_shape, LOCAL)],
            [tok(count)] * 4 + [sq(count), sq(count), tok(count), tok(count, LOCAL), tok(count, LOCAL),
                                square, square, column(BF16)] + SCALARS + [sems(2), sems(9, count)],
            4 * unit * count // n, 20 * MB * count // n,
            alias={9 + j: j for j in range(len(earlier))},
        )(lens, d_att, queries, keys, values, carry_in, early, mask, mask_t, *earlier)

    partial = gradients(0, BACK_SPLIT)
    gg_shape = (GG_ROWS // 2, HD)
    back_sum, gg_mine = call(
        scan_back_kernel, "scan_back", [ANY] * 2, [ANY, NEAR],
        [struct(slices, BF16), struct(gg_shape, F32)],
        [scan_buf, scan_buf, near((N_SEQ, GG_ROWS, HD), BF16)] + SCALARS + [sems(3, parts)], MB, MB,
        grant=SMALL_GRANT,
    )(lens, back)
    back_sum, gg_mine, *partial = lax.optimization_barrier((back_sum, gg_mine, *partial))
    carry_back = swap(back_sum).reshape(state_shape)
    gg_other = exchange(gg_mine, "dp")
    grad_queries, gk_local, gv_local = gradients(BACK_SPLIT, n - BACK_SPLIT, *partial)
    grad_keys, grad_values, grad_gain = call(
        close_kernel, "close", [ANY] * 7 + [NEAR] * 2, [ANY, ANY, NEAR],
        [wide, wide, struct(gg_shape, F32)],
        [tok(n, LOCAL), tok(n, LOCAL), tok(n), tok(n), sq(n), sq(n), tok(n), tok(n), column(BF16)]
        + SCALARS + [sems(8, n)], unit // 2, 17 * MB, grant=PART_GRANT,
    )(lens, gk_local, gv_local, keys, values, carry_back, late, gg_mine, gg_other)
    return layer_out, grad_queries, grad_keys, grad_values, grad_gain.reshape(width)


def solution(mesh):
    spread = P("dp", "seq", "tensor")
    return jax.shard_map(
        body, mesh=mesh,
        in_specs=(spread, spread, spread, spread, P("dp", None), P("tensor")),
        out_specs=(spread, spread, spread, spread, P("tensor")),
        check_vma=False,
    )
```

time: 550 us -> 107 us (0.19)
  blocking collectives: 332 us -> 0 us
  other arithmetic: 103 us -> 0 us
  Pallas kernels: 0 us -> 61.9 us
  matrix products: 50.3 us -> 0 us
  local copies, waits for them, and re-layouts: 44.8 us -> 0.03 us
  starting transfers between devices: 0.08 us -> 26 us
  waiting for transfers between devices: 0.04 us -> 16.5 us
  between operations: 16.2 us -> 0.96 us
    psum x3 -> x0, blocking collectives: 262 us -> none  [the longest x1 252 us: body(): grad_gain = lax.psum(jnp.sum(upstream * unit, axis=0), ('dp', 'seq'))]
    unnamed x1 -> x0, blocking collectives: 69.2 us -> none
    add x32 -> x0, other arithmetic: 65.4 us -> none  [the longest x31 65.4 us: linked(): return (later[0] + keeping * earlier[0], jnp.maximum(earlier[1], later[1]))]
    pallas_call x0 -> x10, Pallas kernels: none -> 61.9 us  [the longest x2 19.5 us: gradients(): call(kernel, f'grad_from_{first}', [HBM] * (9 + len(earlier)), [HBM] * 3,...]
    dot_general x12 -> x0, matrix products: 50.3 us -> none  [the longest x1 6.69 us: body(): jnp.einsum('hts,htd->hsd', d_scores, query, preferred_element_type=jnp.fl...]
    unnamed x33 -> x12, local copies, waits for them, and re-layouts: 28.3 us -> 0.03 us
    sub x32 -> x0, other arithmetic: 20.3 us -> none  [the longest x31 20.3 us: linked(): keeping = 1.0 - later[1][0]]
    all_to_all x0 -> x4, starting transfers between devices: none -> 19.9 us  [swap(): return lax.all_to_all(x, 'seq', 0, 0, tiled=True)]
  transfers between devices with their start and end apart: 2 -> 6, of which waited for: 0 -> 4; matrix products, arithmetic and copies ran while one was open for 10% -> 0% of each run, Pallas kernels for 0% -> 29%
where the time goes in v2:
time: 107 us; the launch traced here: 105 us
  Pallas kernels  61.9 us (58%)
  starting transfers between devices  26 us (24%)
  waiting for transfers between devices  16.5 us (15%)
    all_to_all x4, starting transfers between devices, swap(): return lax.all_to_all(x, 'seq', 0, 0, tiled=True)  19.9 us
    pallas_call x2, Pallas kernels, gradients(): call(kernel, f'grad_from_{first}', [HBM] * (9 + len(earlier)), [HBM] * 3,...  19.5 us
    all_to_all x4, waiting for transfers between devices, swap(): return lax.all_to_all(x, 'seq', 0, 0, tiled=True)  14.7 us
    pallas_call x1, Pallas kernels, body(): call(norm_kernel, 'norm', [ANY] + [NEAR] * 2 + [ANY] * 5 + [NEAR], [ANY]...  10.6 us
    pallas_call x1, Pallas kernels, body(): call(close_kernel, 'close', [ANY] * 7 + [NEAR] * 2, [ANY, ANY, NEAR], [wi...  7.5 us
    ppermute x2, starting transfers between devices, exchange(): return lax.ppermute(x, axis, [(0, 1), (1, 0)])  6.14 us
    pallas_call x1, Pallas kernels, body(): call(attend_second_kernel, 'attend_second', [HBM] * 5, HBM, struct(head_s...  5.78 us
    pallas_call x1, Pallas kernels, body(): call(attend_first_kernel, 'attend_first', [HBM] * 4, [HBM] * 3, [struct(h...  5.44 us
  transfers between devices with their start and end apart: 6, of which 4 were waited for; matrix products, arithmetic and copies ran while one was open for 0% of the time, Pallas kernels for 29%

profile of v2, /device:TPU:0, one launch (start us, length us, event | category | flops | bytes accessed | tf_op | source)
XLA Modules:
  0.0 105.4 jit_solution(13346192029839489037)
XLA Ops:
  0.6 4.6 %state.1 = (bf16[2048,128]{1,0:T(8,128)(2,1)}, bf16[2048,128]{1,0:T(8,128)(2,1)}) custom-call(s32[1,16]{1,0:T(1,128)} %lens.13, bf16[1,512,2048]{2,1,0:T(8,128)(2,1)} %k.7, bf16[1,512,2048]{2,1,0:T(8,128)(2,1)} %v.7), custom_call_target="tpu_custom_call" | custom-call | flops 268435456 | bytes 5242880 | tf_op jit(solution)/shard_map/state/pallas_call | solution.py:490
  5.2 7.4 %all-to-all-start = ((bf16[32,64,128]{2,1,0:T(8,128)(2,1)}), bf16[32,64,128]{2,1,0:T(8,128)(2,1)S(1)}, u32[]{:S(2)}, u32[]{:S(2)}) async-start(bf16[32,64,128]{2,1,0:T(8,128)(2,1)} %bitcast.12), calls=%async_computation | async-start | bytes 1048576 | tf_op jit(solution)/shard_map/all_to_all | solution.py:469
  12.7 0.0 copy-start.2
  12.7 5.4 %attend_first.1 = (bf16[16,512,128]{2,1,0:T(8,128)(2,1)}, bf16[512,256]{1,0:T(8,128)(2,1)}, bf16[512,256]{1,0:T(8,128)(2,1)}) custom-call(s32[1,16]{1,0:T(1,128)} %lens.13, bf16[1,512,2048]{2,1,0:T(8,128)(2,1)} %refs_2_.3, bf16[1,512,2048]{2,1,0:T(8,128)(2,1)} %k.7, bf16[1,512,2048]{2,1,0:T(8,128)(2,1)} %v.7), custom_call_target="tpu_custom_call" | custom-call | flops 1073741824 | bytes 6291456 | tf_op jit(solution)/shard_map/attend_first/pallas_call | solution.py:495
  18.1 6.1 %all-to-all-done.x = bf16[32,64,128]{2,1,0:T(8,128)(2,1)S(1)} async-done(((bf16[32,64,128]{2,1,0:T(8,128)(2,1)}), bf16[32,64,128]{2,1,0:T(8,128)(2,1)S(1)}, u32[]{:S(2)}, u32[]{:S(2)}) %all-to-all-start) | async-done | bytes 524320 | tf_op jit(solution)/shard_map/all_to_all | solution.py:469
  24.3 0.0 copy-done.2
  24.3 1.6 %scan.1 = bf16[32,64,128]{2,1,0:T(8,128)(2,1)} custom-call(s32[1,16]{1,0:T(1,128)S(1)} %copy-done.2, bf16[32,64,128]{2,1,0:T(8,128)(2,1)S(1)} %all-to-all-done.x), custom_call_target="tpu_custom_call" | custom-call | flops 1048576 | bytes 1048576 | tf_op jit(solution)/shard_map/scan/pallas_call | solution.py:501
  25.9 3.9 %all-to-all-start.1 = ((bf16[32,64,128]{2,1,0:T(8,128)(2,1)}), bf16[32,64,128]{2,1,0:T(8,128)(2,1)S(1)}, u32[]{:S(2)}, u32[]{:S(2)}) async-start(bf16[32,64,128]{2,1,0:T(8,128)(2,1)} %scan.1), calls=%async_computation.1 | async-start | bytes 1048576 | tf_op jit(solution)/shard_map/all_to_all | solution.py:469
  29.8 0.0 copy-start.1
  29.8 0.0 copy-start.5
  29.8 5.8 %attend_second.1.local = bf16[16,512,128]{2,1,0:T(8,128)(2,1)} custom-call(bf16[1,512,2048]{2,1,0:T(8,128)(2,1)} %refs_2_.3, bf16[1,512,2048]{2,1,0:T(8,128)(2,1)} %k.7, bf16[1,512,2048]{2,1,0:T(8,128)(2,1)} %v.7, bf16[512,256]{1,0:T(8,128)(2,1)} %get-tuple-element.32.mask_in.refs_7_, ...), custom_call_target="tpu_custom_call", output_to_operand_aliasing={{}: (4, {})} | custom-call | flops 1073741824 | bytes 6291456 | tf_op jit(solution)/shard_map/attend_second/pallas_call | solution.py:507
  35.6 5.8 %all-to-all-done.1 = bf16[32,64,128]{2,1,0:T(8,128)(2,1)S(1)} async-done(((bf16[32,64,128]{2,1,0:T(8,128)(2,1)}), bf16[32,64,128]{2,1,0:T(8,128)(2,1)S(1)}, u32[]{:S(2)}, u32[]{:S(2)}) %all-to-all-start.1) | async-done | bytes 524320 | tf_op jit(solution)/shard_map/all_to_all | solution.py:469
  41.4 0.0 copy-done.1
  41.4 0.0 copy-done.5
  41.4 5.2 %sums.1.mine = f32[8,512]{1,0:T(8,128)S(1)} custom-call(s32[1,16]{1,0:T(1,128)S(1)} %copy-done.2, bf16[16,512,128]{2,1,0:T(8,128)(2,1)} %attend_second.1.local, bf16[1,512,2048]{2,1,0:T(8,128)(2,1)} %refs_2_.3, bf16[2048,128]{1,0:T(8,128)(2,1)S(1)} %bitcast.5, bf16[2048,128]{1,0:T(8,128)(2,1)S(1)} %copy-done.1, bf16[1,512,2048]{2,1,0:T(8,128)(2,1)} %up.3, ...), custom_call_target="tpu_custom_call" | custom-call | flops 268435456 | bytes 9437184 | tf_op jit(solution)/shard_map/sums/pallas_call | solution.py:512
  46.6 2.0 %collective-permute-start = (f32[8,512]{1,0:T(8,128)S(1)}, f32[8,512]{1,0:T(8,128)S(1)}, u32[]{:S(2)}, u32[]{:S(2)}) collective-permute-start(f32[8,512]{1,0:T(8,128)S(1)} %sums.1.mine), channel_id=1, source_target_pairs={{0,1},{1,0},{2,3},{3,2},{4,5},{5,4},{6,7},{7,6},{8,9},{9,8},{10,11... | collective-permute-start | bytes 49160 | tf_op jit(solution)/shard_map/ppermute | solution.py:465
  48.6 1.8 %collective-permute-done.other = f32[8,512]{1,0:T(8,128)S(1)} collective-permute-done((f32[8,512]{1,0:T(8,128)S(1)}, f32[8,512]{1,0:T(8,128)S(1)}, u32[]{:S(2)}, u32[]{:S(2)}) %collective-permute-start) | collective-permute-done | bytes 16416 | tf_op jit(solution)/shard_map/ppermute | solution.py:465
  50.4 0.0 copy-done
  50.4 10.6 %norm.1 = (bf16[1,512,2048]{2,1,0:T(8,128)(2,1)}, bf16[16,512,128]{2,1,0:T(8,128)(2,1)}, bf16[32,96,128]{2,1,0:T(8,128)(2,1)}, bf16[2048,128]{1,0:T(8,128)(2,1)S(1)}) custom-call(s32[1,16]{1,0:T(1,128)S(1)} %copy-done.2, f32[8,512]{1,0:T(8,128)S(1)} %sums.1.mine, f32[8,512]{1,0:T(8,128)S(1)} %collective-permute-done.other, ...), custom_call_target="tpu_custom_call" | custom-call | flops 536870912 | bytes 13631488 | tf_op jit(solution)/shard_map/norm/pallas_call | solution.py:519
  61.0 3.9 %all-to-all-start.2 = ((bf16[32,96,128]{2,1,0:T(8,128)(2,1)}), bf16[32,96,128]{2,1,0:T(8,128)(2,1)S(1)}, u32[]{:S(2)}, u32[]{:S(2)}) async-start(bf16[32,96,128]{2,1,0:T(8,128)(2,1)} %get-tuple-element.41), calls=%async_computation.2 | async-start | bytes 1572864 | tf_op jit(solution)/shard_map/all_to_all | solution.py:469
  64.9 0.0 copy-start.3
  64.9 11.7 %grad_from_0.1 = (bf16[1,512,2048]{2,1,0:T(8,128)(2,1)}, bf16[16,512,128]{2,1,0:T(8,128)(2,1)}, bf16[16,512,128]{2,1,0:T(8,128)(2,1)}) custom-call(s32[1,16]{1,0:T(1,128)} %lens.13, bf16[16,512,128]{2,1,0:T(8,128)(2,1)} %get-tuple-element.39.refs_1_, bf16[1,512,2048]{2,1,0:T(8,128)(2,1)} %refs_2_.3, bf16[1,512,2048]{2,1,0:T(8,128)(2,1)} %k.7, ...), custom_call_target="tpu_custom_call" | custom-call | flops 2684354560 | bytes 13107200 | tf_op jit(solution)/shard_map/grad_from_0/pallas_call | solution.py:532
  76.6 2.8 %all-to-all-done.2.x = bf16[32,96,128]{2,1,0:T(8,128)(2,1)S(1)} async-done(((bf16[32,96,128]{2,1,0:T(8,128)(2,1)}), bf16[32,96,128]{2,1,0:T(8,128)(2,1)S(1)}, u32[]{:S(2)}, u32[]{:S(2)}) %all-to-all-start.2) | async-done | bytes 786464 | tf_op jit(solution)/shard_map/all_to_all | solution.py:469
  79.4 1.7 %scan_back.1 = (bf16[32,64,128]{2,1,0:T(8,128)(2,1)}, f32[16,128]{1,0:T(8,128)S(1)}) custom-call(s32[1,16]{1,0:T(1,128)S(1)} %copy-done.3, bf16[32,96,128]{2,1,0:T(8,128)(2,1)S(1)} %all-to-all-done.2.x), custom_call_target="tpu_custom_call" | custom-call | flops 1048576 | bytes 1048576 | tf_op jit(solution)/shard_map/scan_back/pallas_call | solution.py:543
  81.1 4.6 %all-to-all-start.3 = ((bf16[32,64,128]{2,1,0:T(8,128)(2,1)}), bf16[32,64,128]{2,1,0:T(8,128)(2,1)S(1)}, u32[]{:S(2)}, u32[]{:S(2)}) async-start(bf16[32,64,128]{2,1,0:T(8,128)(2,1)} %get-tuple-element.53), calls=%async_computation.3 | async-start | bytes 1048576 | tf_op jit(solution)/shard_map/all_to_all | solution.py:469
  85.7 0.0 copy-start.4
  85.8 4.1 %collective-permute-start.1 = (f32[16,128]{1,0:T(8,128)S(1)}, f32[16,128]{1,0:T(8,128)S(1)}, u32[]{:S(2)}, u32[]{:S(2)}) collective-permute-start(f32[16,128]{1,0:T(8,128)S(1)} %get-tuple-element.55.gg_mine), channel_id=1, source_target_pairs={{0,64},{64,0},{1,65},{65,1},{2,66},{66,2},{3,67},{67,3},{4,68},{68... | collective-permute-start | bytes 24584 | tf_op jit(solution)/shard_map/ppermute | solution.py:465
  89.9 7.8 %grad_from_10.1 = (bf16[1,512,2048]{2,1,0:T(8,128)(2,1)}, bf16[16,512,128]{2,1,0:T(8,128)(2,1)}, bf16[16,512,128]{2,1,0:T(8,128)(2,1)}) custom-call(s32[1,16]{1,0:T(1,128)} %lens.13, bf16[16,512,128]{2,1,0:T(8,128)(2,1)} %get-tuple-element.39.refs_1_, bf16[1,512,2048]{2,1,0:T(8,128)(2,1)} %refs_2_.3, ...), custom_call_target="tpu_custom_call", output_to_operand_aliasing={{0}: (9, {}), {1}: (10, {}), {2}: (11, {})} | custom-call | flops 1610612736 | bytes 7864320 | tf_op jit(solution)/shard_map/grad_from_10/pallas_call | solution.py:532
  97.7 0.0 collective-permute-done.1.gg_other
  97.7 0.0 all-to-all-done.3
  97.7 0.0 copy-done.4
  97.8 7.5 %close.1 = (bf16[1,512,2048]{2,1,0:T(8,128)(2,1)}, bf16[1,512,2048]{2,1,0:T(8,128)(2,1)}, f32[16,128]{1,0:T(8,128)}) custom-call(s32[1,16]{1,0:T(1,128)S(1)} %copy-done.4, bf16[16,512,128]{2,1,0:T(8,128)(2,1)} %get-tuple-element.51.gk_local, bf16[16,512,128]{2,1,0:T(8,128)(2,1)} %get-tuple-element.52.gv_local, bf16[1,512,2048]{2,1,0:T(8,128)(2,1)} %k.7, ...), custom_call_target="tpu_custom_call" | custom-call | flops 536870912 | bytes 17825792 | tf_op jit(solution)/shard_map/close/pallas_call | solution.py:553
  (2 shorter events, 0.0 us)
Async XLA Ops:
  5.2 19.0 %all-to-all-start = ((bf16[32,64,128]{2,1,0:T(8,128)(2,1)}), bf16[32,64,128]{2,1,0:T(8,128)(2,1)S(1)}, u32[]{:S(2)}, u32[]{:S(2)}) async-start(bf16[32,64,128]{2,1,0:T(8,128)(2,1)} %bitcast.12), calls=%async_computation | async-start | bytes 1048576 | tf_op jit(solution)/shard_map/all_to_all | solution.py:469
  12.7 11.6 %copy-start.2 = (s32[1,16]{1,0:T(1,128)S(1)}, s32[1,16]{1,0:T(1,128)}, u32[]{:S(2)}) copy-start(s32[1,16]{1,0:T(1,128)} %lens.13) | copy-start | bytes 196
  25.9 15.5 %all-to-all-start.1 = ((bf16[32,64,128]{2,1,0:T(8,128)(2,1)}), bf16[32,64,128]{2,1,0:T(8,128)(2,1)S(1)}, u32[]{:S(2)}, u32[]{:S(2)}) async-start(bf16[32,64,128]{2,1,0:T(8,128)(2,1)} %scan.1), calls=%async_computation.1 | async-start | bytes 1048576 | tf_op jit(solution)/shard_map/all_to_all | solution.py:469
  29.8 11.6 %copy-start.1 = (bf16[2048,128]{1,0:T(8,128)(2,1)S(1)}, bf16[2048,128]{1,0:T(8,128)(2,1)}, u32[]{:S(2)}) copy-start(bf16[2048,128]{1,0:T(8,128)(2,1)} %get-tuple-element.37.early.refs_6_) | copy-start | bytes 1572868
  29.8 11.6 %copy-start.5 = (f32[2048]{0:T(1024)S(1)}, f32[2048]{0:T(1024)}, u32[]{:S(2)}) copy-start(f32[2048]{0:T(1024)} %param.11) | copy-start | bytes 24580
  41.4 9.0 %copy-start = (bf16[32,64,128]{2,1,0:T(8,128)(2,1)}, bf16[32,64,128]{2,1,0:T(8,128)(2,1)S(1)}, u32[]{:S(2)}) copy-start(bf16[32,64,128]{2,1,0:T(8,128)(2,1)S(1)} %all-to-all-done.1) | copy-start | bytes 1572868
  46.6 3.8 %collective-permute-start = (f32[8,512]{1,0:T(8,128)S(1)}, f32[8,512]{1,0:T(8,128)S(1)}, u32[]{:S(2)}, u32[]{:S(2)}) collective-permute-start(f32[8,512]{1,0:T(8,128)S(1)} %sums.1.mine), channel_id=1, source_target_pairs={{0,1},{1,0},{2,3},{3,2},{4,5},{5,4},{6,7},{7,6},{8,9},{9,8},{10,11... | collective-permute-start | bytes 49160 | tf_op jit(solution)/shard_map/ppermute | solution.py:465
  61.0 18.5 %all-to-all-start.2 = ((bf16[32,96,128]{2,1,0:T(8,128)(2,1)}), bf16[32,96,128]{2,1,0:T(8,128)(2,1)S(1)}, u32[]{:S(2)}, u32[]{:S(2)}) async-start(bf16[32,96,128]{2,1,0:T(8,128)(2,1)} %get-tuple-element.41), calls=%async_computation.2 | async-start | bytes 1572864 | tf_op jit(solution)/shard_map/all_to_all | solution.py:469
  64.9 14.5 %copy-start.3 = (s32[1,16]{1,0:T(1,128)S(1)}, s32[1,16]{1,0:T(1,128)}, u32[]{:S(2)}) copy-start(s32[1,16]{1,0:T(1,128)} %lens.13) | copy-start | bytes 196
  81.1 16.6 %all-to-all-start.3 = ((bf16[32,64,128]{2,1,0:T(8,128)(2,1)}), bf16[32,64,128]{2,1,0:T(8,128)(2,1)S(1)}, u32[]{:S(2)}, u32[]{:S(2)}) async-start(bf16[32,64,128]{2,1,0:T(8,128)(2,1)} %get-tuple-element.53), calls=%async_computation.3 | async-start | bytes 1048576 | tf_op jit(solution)/shard_map/all_to_all | solution.py:469
  85.7 12.0 %copy-start.4 = (s32[1,16]{1,0:T(1,128)S(1)}, s32[1,16]{1,0:T(1,128)}, u32[]{:S(2)}) copy-start(s32[1,16]{1,0:T(1,128)} %lens.13) | copy-start | bytes 196
  85.8 12.0 %collective-permute-start.1 = (f32[16,128]{1,0:T(8,128)S(1)}, f32[16,128]{1,0:T(8,128)S(1)}, u32[]{:S(2)}, u32[]{:S(2)}) collective-permute-start(f32[16,128]{1,0:T(8,128)S(1)} %get-tuple-element.55.gg_mine), channel_id=1, source_target_pairs={{0,64},{64,0},{1,65},{65,1},{2,66},{66,2},{3,67},{67,3},{4,68},{68... | collective-permute-start | bytes 24584 | tf_op jit(solution)/shard_map/ppermute | solution.py:465
